TPU v7x, 256 devices: a whole 4x4x8 slice. The times are simulated.
256 devices in a mesh: cluster: 8 (over z_hi, core), shard: 32 (over x, z_lo, y).
Axes of the slice: x: 4, y: 4, z: 8 (z_hi: 4, z_lo: 2; z = z_hi * 2 + z_lo), core: 2. Of those that a mesh axis runs over, the one named last changes fastest.
Arguments:
- flow_start: float32 [4096, 256], P(('cluster', 'shard')), may hold values from 0 to 1
- demand: float32 [4096, 256], P(('cluster', 'shard')), may hold values from 0.25 to 2
- utility: float32 [4096, 256], P(('cluster', 'shard')), may hold values from 1 to 16
- path_count: int32 [4096], P(('cluster', 'shard')), may hold values from 1 to 256, as said below
- cluster_size: int32 [8], P('cluster'), may hold values from 1 to 16, as said below
- incidence: float32 [8192, 256, 128], P(('cluster', 'shard')), may hold values from 0 to 1, as said below
- inc_path: int32 [8192], P(('cluster', 'shard')), may hold values from 0 to 511, as said below
- inc_edge: int32 [8192], P(('cluster', 'shard')), may hold values from 0 to 6
- capacity: float32 [1792, 128], P(('cluster', 'shard')), may hold values from 0.25 to 4
- dual_start: float32 [1792, 128], P(('cluster', 'shard')), may hold values from 0 to 7
- partner: int32 [8, 3], P('cluster'), may hold values from 0 to 7, as said below
Outputs:
- flows: float32 [4096, 256], P(('cluster', 'shard'))
- duals: float32 [1792, 128], P(('cluster', 'shard'))
Inputs may be any that keep to these rules, and one draw needn't show every extreme that they name: `path_count`: some path block has 256 live paths. `cluster_size`: some cluster has 16. partner[c, k] = q implies partner[q, k] = c; the partners of a cluster are distinct and differ from it. `incidence`: every entry is 0 or 1. Among the 32 incidence blocks of one device, at most 2 have the same value of inc_path // 16, and on every device some value is taken by exactly 2.
All inputs are finite; a program needn't handle non-finite values.
Results may differ from a plain program's by a relative error of at most 0.0001.
Values sent between devices are 32-bit elements; how exact they have to be, the bound alone decides.
A program may use at most 64 MiB of HBM per device.

v0:
```python
import jax
import jax.numpy as jnp
from jax import lax
from jax.sharding import PartitionSpec as P

ITERS = 3


def body(
    flow_start,
    demand,
    utility,
    path_count,
    cluster_size,
    incidence,
    inc_path,
    inc_edge,
    capacity,
    dual_start,
    partner,
):
    exact_mode = lax.Precision.HIGHEST
    block_count, path_width = flow_start.shape
    inc_count = incidence.shape[0]
    edge_width = incidence.shape[2]
    local_blocks = capacity.shape[0]
    slot_count = partner.shape[1]
    interior = local_blocks - slot_count
    clusters = lax.axis_size("cluster")
    norm_bound = max(
        2, inc_count * inc_count * path_width * edge_width // (1024 * local_blocks * block_count)
    )
    capacity_unit = float(max(1, inc_count * path_width // (160 * local_blocks)))
    step_size = 1.0 / (2.0 * norm_bound)
    block_ids = jnp.arange(block_count, dtype=jnp.int32)
    path_ids = jnp.arange(path_width, dtype=jnp.int32)
    live_mask = (
        (block_ids < cluster_size[0])[:, None] & (path_ids[None, :] < path_count[:, None])
    ).astype(jnp.float32)
    edge_pick = (jnp.arange(local_blocks, dtype=jnp.int32)[:, None] == inc_edge[None, :]).astype(
        jnp.float32
    )
    partner_pick = (jnp.arange(clusters, dtype=jnp.int32)[:, None] == partner[0][None, :]).astype(
        jnp.float32
    )

    def twin_of(border):
        outgoing = jnp.dot(partner_pick, border, precision=exact_mode)
        incoming = lax.all_to_all(outgoing, "cluster", split_axis=0, concat_axis=0, tiled=True)
        return jnp.dot(partner_pick.T, incoming, precision=exact_mode)

    cap_border = capacity[interior:]
    dual_border = dual_start[interior:]
    outgoing = jnp.einsum(
        "ck,mke->cme", partner_pick, jnp.stack([cap_border, dual_border]), precision=exact_mode
    )
    incoming = lax.all_to_all(outgoing, "cluster", split_axis=0, concat_axis=0, tiled=True)
    twins = jnp.einsum("ck,cme->mke", partner_pick, incoming, precision=exact_mode)
    limit = capacity_unit * jnp.concatenate(
        [capacity[:interior], 0.5 * (cap_border + twins[0])], axis=0
    )
    duals = jnp.concatenate([dual_start[:interior], 0.5 * (dual_border + twins[1])], axis=0)

    def load_of_rows(picked):
        terms = jnp.einsum("ipe,ip->ie", incidence, picked, precision=exact_mode)
        own_load = jnp.dot(edge_pick, terms, precision=exact_mode)
        border = own_load[interior:]
        return jnp.concatenate([own_load[:interior], border + twin_of(border)], axis=0)

    def total_load(gathered):
        return load_of_rows(jnp.take(gathered, inc_path, axis=0))

    def settle(load, duals_now):
        split = jnp.minimum(limit, load + duals_now)
        return (split, duals_now + load - split)

    flows = jnp.minimum(jnp.maximum(flow_start, 0.0), demand) * live_mask

    def shared_flows(flows_now):
        return lax.all_gather(flows_now, "shard", axis=0, tiled=True)

    load = total_load(shared_flows(flows))
    split, duals = settle(load, duals)
    for iteration in range(ITERS):
        residual = load - split + duals
        residual_picked = jnp.take(residual, inc_edge, axis=0)
        terms = jnp.einsum("ipe,ie->ip", incidence, residual_picked, precision=exact_mode)
        rows_pick = (
            jnp.arange(block_count * lax.axis_size("shard"), dtype=jnp.int32)[:, None]
            == inc_path[None, :]
        ).astype(jnp.float32)
        gradient = lax.psum_scatter(
            jnp.dot(rows_pick, terms, precision=exact_mode),
            "shard",
            scatter_dimension=0,
            tiled=True,
        )
        flows = (
            jnp.minimum(jnp.maximum(flows - step_size * (gradient - utility), 0.0), demand)
            * live_mask
        )
        load = total_load(shared_flows(flows))
        split, duals = settle(load, duals)
    return (flows, duals)


def solution(mesh):
    return jax.shard_map(
        body,
        mesh=mesh,
        in_specs=(
            P(("cluster", "shard"), None),
            P(("cluster", "shard"), None),
            P(("cluster", "shard"), None),
            P(("cluster", "shard")),
            P("cluster"),
            P(("cluster", "shard"), None, None),
            P(("cluster", "shard")),
            P(("cluster", "shard")),
            P(("cluster", "shard"), None),
            P(("cluster", "shard"), None),
            P("cluster", None),
        ),
        out_specs=(P(("cluster", "shard"), None), P(("cluster", "shard"), None)),
        check_vma=False,
    )
```

profile of v0, /device:TPU:1, one launch (start us, length us, event | category | flops | bytes accessed | tf_op | source)
XLA Modules:
  0.0 920.1 jit_solution(6697938760290475055)
XLA Ops:
  7.2 0.7 compare_and_fusion.1
  7.9 0.7 compare_select_fusion.1
  9.2 0.8 minimum_select_fusion.3
  10.0 71.7 %all_gather.12 = f32[512,256]{1,0:T(8,128)S(1)} all-gather(f32[16,256]{1,0:T(8,128)S(1)} %minimum_select_fusion.3), channel_id=1, replica_groups=mesh['cluster'=8,'shard'=32] {'shard'}, dimensions={0}, use_global_device_ids=true | all-gather | bytes 540672 | tf_op jit(solution)/shard_map/all_gather | solution.py:80
  81.8 0.6 gather_fusion
  82.4 0.1 select_bitcast_fusion.3
  82.5 4.4 fusion.18
  86.8 0.1 fusion.29
  87.0 0.9 fusion.39
  87.8 21.9 %all-to-all-start = ((f32[8,1,128]{2,1,0:T(1,128)}), f32[8,1,128]{2,1,0:T(1,128)S(1)}, u32[]{:S(2)}, u32[]{:S(2)}) async-start(f32[8,1,128]{2,1,0:T(1,128)} %bitcast.6), calls=%async_computation | async-start | bytes 8192 | tf_op jit(solution)/shard_map/all_to_all | solution.py:49
  109.8 0.3 fusion.22
  110.1 0.6 copy.20
  110.7 6.0 all-to-all-done
  116.7 3.9 all-to-all-start.1
  120.6 0.2 convolution_add_fusion.3
  120.8 6.9 all-to-all-done.1
  127.6 0.2 convolution_bitcast_fusion
  127.9 0.6 gather_fusion.1
  128.4 0.1 broadcast_select_fusion.2
  128.5 5.7 fusion.61
  134.2 1.2 fusion.2
  135.4 128.4 %reduce-scatter.4.cloned.1.call-done = f32[16,256]{1,0:T(8,128)} async-done(((f32[512,256]{1,0:T(8,128)}), f32[16,256]{1,0:T(8,128)}) %reduce-scatter.4.cloned.1.call-update) | async-done | bytes 16400 | tf_op jit(solution)/shard_map/reduce_scatter | solution.py:92
  263.8 0.8 minimum_select_fusion.2
  264.6 65.2 %all_gather.13 = f32[512,256]{1,0:T(8,128)S(1)} all-gather(f32[16,256]{1,0:T(8,128)S(1)} %minimum_select_fusion.2), channel_id=1, replica_groups=mesh['cluster'=8,'shard'=32] {'shard'}, dimensions={0}, use_global_device_ids=true | all-gather | bytes 540672 | tf_op jit(solution)/shard_map/all_gather | solution.py:80
  329.7 0.6 gather_fusion.2
  330.3 0.1 select_bitcast_fusion.2
  330.4 4.3 fusion.15
  334.7 0.1 fusion.28
  334.9 0.9 fusion.37
  335.7 46.7 %all-to-all-start.2 = ((f32[8,1,128]{2,1,0:T(1,128)}), f32[8,1,128]{2,1,0:T(1,128)S(1)}, u32[]{:S(2)}, u32[]{:S(2)}) async-start(f32[8,1,128]{2,1,0:T(1,128)} %bitcast.21), calls=%async_computation.3 | async-start | bytes 8192 | tf_op jit(solution)/shard_map/all_to_all | solution.py:49
  382.4 6.9 all-to-all-done.2
  389.3 0.2 convolution_add_fusion.2
  389.6 0.6 gather_fusion.3
  390.1 0.1 broadcast_select_fusion.1
  390.2 5.7 fusion.62
  395.9 1.2 fusion.1
  397.1 0.0 reduce-scatter.6.cloned.1.call-update
  397.1 128.4 %reduce-scatter.6.cloned.1.call-done = f32[16,256]{1,0:T(8,128)} async-done(((f32[512,256]{1,0:T(8,128)}), f32[16,256]{1,0:T(8,128)}) %reduce-scatter.6.cloned.1.call-update) | async-done | bytes 16400 | tf_op jit(solution)/shard_map/reduce_scatter | solution.py:92
  525.5 0.8 minimum_select_fusion.1
  526.2 65.5 %all_gather.14 = f32[512,256]{1,0:T(8,128)S(1)} all-gather(f32[16,256]{1,0:T(8,128)S(1)} %minimum_select_fusion.1), channel_id=1, replica_groups=mesh['cluster'=8,'shard'=32] {'shard'}, dimensions={0}, use_global_device_ids=true | all-gather | bytes 540672 | tf_op jit(solution)/shard_map/all_gather | solution.py:80
  591.7 0.6 gather_fusion.4
  592.3 0.1 select_bitcast_fusion.1
  592.4 4.3 fusion.12
  596.7 0.1 fusion.27
  596.8 0.9 fusion.36
  597.7 46.2 %all-to-all-start.3 = ((f32[8,1,128]{2,1,0:T(1,128)}), f32[8,1,128]{2,1,0:T(1,128)S(1)}, u32[]{:S(2)}, u32[]{:S(2)}) async-start(f32[8,1,128]{2,1,0:T(1,128)} %bitcast.30), calls=%async_computation.5 | async-start | bytes 8192 | tf_op jit(solution)/shard_map/all_to_all | solution.py:49
  643.9 6.9 all-to-all-done.3
  650.9 0.2 convolution_add_fusion.1
  651.1 0.6 gather_fusion.5
  651.6 0.1 broadcast_select_fusion
  651.7 5.7 fusion.63
  657.4 1.2 fusion
  658.6 128.6 %reduce-scatter.8.cloned.1.call-done = f32[16,256]{1,0:T(8,128)} async-done(((f32[512,256]{1,0:T(8,128)}), f32[16,256]{1,0:T(8,128)}) %reduce-scatter.8.cloned.1.call-update) | async-done | bytes 16400 | tf_op jit(solution)/shard_map/reduce_scatter | solution.py:92
  787.2 0.8 minimum_select_fusion
  788.0 65.5 %all_gather.15 = f32[512,256]{1,0:T(8,128)S(1)} all-gather(f32[16,256]{1,0:T(8,128)S(1)} %minimum_select_fusion), channel_id=1, replica_groups=mesh['cluster'=8,'shard'=32] {'shard'}, dimensions={0}, use_global_device_ids=true | all-gather | bytes 540672 | tf_op jit(solution)/shard_map/all_gather | solution.py:80
  853.5 0.6 gather_fusion.6
  854.1 0.1 select_bitcast_fusion
  854.2 4.3 fusion.9
  858.5 0.1 fusion.26
  858.6 0.9 fusion.35
  859.5 46.3 %all-to-all-start.4 = ((f32[8,1,128]{2,1,0:T(1,128)}), f32[8,1,128]{2,1,0:T(1,128)S(1)}, u32[]{:S(2)}, u32[]{:S(2)}) async-start(f32[8,1,128]{2,1,0:T(1,128)} %bitcast.39), calls=%async_computation.7 | async-start | bytes 8192 | tf_op jit(solution)/shard_map/all_to_all | solution.py:49
  905.8 6.9 all-to-all-done.4
  912.7 0.2 convolution_add_fusion
  912.9 0.6 minimum_subtract_fusion
  (41 shorter events, 0.2 us)
Async XLA Ops:
  7.2 79.7 %copy-start.6 = (s32[32]{0:T(128)S(1)}, s32[32]{0:T(128)}, u32[]{:S(2)}) copy-start(s32[32]{0:T(128)} %param.22) | copy-start | bytes 388
  7.2 79.8 %copy-start.9 = (s32[1,3]{1,0:T(1,128)S(1)}, s32[1,3]{1,0:T(1,128)}, u32[]{:S(2)}) copy-start(s32[1,3]{1,0:T(1,128)} %param.25) | copy-start | bytes 40
  7.2 102.6 %copy-start.4 = (f32[7,128]{1,0:T(8,128)S(1)}, f32[7,128]{1,0:T(8,128)}, u32[]{:S(2)}) copy-start(f32[7,128]{1,0:T(8,128)} %param.24) | copy-start | bytes 10756
  7.2 102.6 %copy-start.5 = (f32[7,128]{1,0:T(8,128)S(1)}, f32[7,128]{1,0:T(8,128)}, u32[]{:S(2)}) copy-start(f32[7,128]{1,0:T(8,128)} %param.23) | copy-start | bytes 10756
  82.5 51.7 %copy-start.8 = (s32[32]{0:T(128)S(1)}, s32[32]{0:T(128)}, u32[]{:S(2)}) copy-start(s32[32]{0:T(128)} %param.21) | copy-start | bytes 388
  82.5 181.3 %copy-start = (f32[16,256]{1,0:T(8,128)S(1)}, f32[16,256]{1,0:T(8,128)}, u32[]{:S(2)}) copy-start(f32[16,256]{1,0:T(8,128)} %param.16) | copy-start | bytes 49156
  82.5 181.3 %copy-start.1 = (f32[16,256]{1,0:T(8,128)S(1)}, f32[16,256]{1,0:T(8,128)}, u32[]{:S(2)}) copy-start(f32[16,256]{1,0:T(8,128)} %param.17) | copy-start | bytes 49156
  82.5 181.3 %copy-start.2 = (f32[16,256]{1,0:T(8,128)S(1)}, f32[16,256]{1,0:T(8,128)}, u32[]{:S(2)}) copy-start(f32[16,256]{1,0:T(8,128)} %param.15) | copy-start | bytes 49156
  82.5 181.3 %copy-start.7 = (s32[16]{0:T(128)S(1)}, s32[16]{0:T(128)}, u32[]{:S(2)}) copy-start(s32[16]{0:T(128)} %param.18) | copy-start | bytes 196
  87.8 28.8 %all-to-all-start = ((f32[8,1,128]{2,1,0:T(1,128)}), f32[8,1,128]{2,1,0:T(1,128)S(1)}, u32[]{:S(2)}, u32[]{:S(2)}) async-start(f32[8,1,128]{2,1,0:T(1,128)} %bitcast.6), calls=%async_computation | async-start | bytes 8192 | tf_op jit(solution)/shard_map/all_to_all | solution.py:49
  116.7 11.0 %all-to-all-start.1 = ((f32[8,2,128]{2,1,0:T(2,128)}), f32[8,2,128]{2,1,0:T(2,128)S(1)}, u32[]{:S(2)}, u32[]{:S(2)}) async-start(f32[8,2,128]{2,1,0:T(2,128)} %copy.20), calls=%async_computation.1 | async-start | bytes 16384 | tf_op jit(solution)/shard_map/all_to_all | solution.py:57
  120.6 143.2 %reduce-scatter.4.cloned.1.call-start = ((), (), s32[]{:S(2)}) async-start(), calls=%async_computation.8 | async-start | bytes 540672 | tf_op jit(solution)/shard_map/reduce_scatter | solution.py:92
  335.7 53.6 %all-to-all-start.2 = ((f32[8,1,128]{2,1,0:T(1,128)}), f32[8,1,128]{2,1,0:T(1,128)S(1)}, u32[]{:S(2)}, u32[]{:S(2)}) async-start(f32[8,1,128]{2,1,0:T(1,128)} %bitcast.21), calls=%async_computation.3 | async-start | bytes 8192 | tf_op jit(solution)/shard_map/all_to_all | solution.py:49
  382.4 143.0 %reduce-scatter.6.cloned.1.call-start = ((), (), s32[]{:S(2)}) async-start(), calls=%async_computation.9 | async-start | bytes 540672 | tf_op jit(solution)/shard_map/reduce_scatter | solution.py:92
  597.7 53.1 %all-to-all-start.3 = ((f32[8,1,128]{2,1,0:T(1,128)}), f32[8,1,128]{2,1,0:T(1,128)S(1)}, u32[]{:S(2)}, u32[]{:S(2)}) async-start(f32[8,1,128]{2,1,0:T(1,128)} %bitcast.30), calls=%async_computation.5 | async-start | bytes 8192 | tf_op jit(solution)/shard_map/all_to_all | solution.py:49
  643.9 143.2 %reduce-scatter.8.cloned.1.call-start = ((), (), s32[]{:S(2)}) async-start(), calls=%async_computation.10 | async-start | bytes 540672 | tf_op jit(solution)/shard_map/reduce_scatter | solution.py:92
  788.0 125.6 %copy-start.3 = (f32[16,256]{1,0:T(8,128)}, f32[16,256]{1,0:T(8,128)S(1)}, u32[]{:S(2)}) copy-start(f32[16,256]{1,0:T(8,128)S(1)} %minimum_select_fusion) | copy-start | bytes 49156
  859.5 53.3 %all-to-all-start.4 = ((f32[8,1,128]{2,1,0:T(1,128)}), f32[8,1,128]{2,1,0:T(1,128)S(1)}, u32[]{:S(2)}, u32[]{:S(2)}) async-start(f32[8,1,128]{2,1,0:T(1,128)} %bitcast.39), calls=%async_computation.7 | async-start | bytes 8192 | tf_op jit(solution)/shard_map/all_to_all | solution.py:49
Sparse Core Ops, SparseCore 0:
  135.5 128.1 reduce-scatter.3
  397.2 128.2 reduce-scatter.5
  658.7 128.3 reduce-scatter.7
where the time goes:
time: 921 us; the launch traced here: 920 us
  waiting for transfers between devices  419 us (45%)
  blocking collectives  268 us (29%)
  starting transfers between devices  165 us (18%)
  matrix products  43 us (5%)
  between operations  14.6 us (2%)
    reduce_scatter x3, waiting for transfers between devices, body(): lax.psum_scatter(jnp.dot(rows_pick, terms, precision=exact_mode), 'shard'...  385 us
    all_gather x4, blocking collectives, shared_flows(): return lax.all_gather(flows_now, 'shard', axis=0, tiled=True)  268 us
    all_to_all x4, starting transfers between devices, twin_of(): lax.all_to_all(outgoing, 'cluster', split_axis=0, concat_axis=0, tiled=True)  161 us
    all_to_all x4, waiting for transfers between devices, twin_of(): lax.all_to_all(outgoing, 'cluster', split_axis=0, concat_axis=0, tiled=True)  26.7 us
  transfers between devices with their start and end apart: 8, of which 8 were waited for; matrix products, arithmetic and copies ran while one was open for 0% of the time, Pallas kernels for 0%

commit v1 on v0

v1 whole, which is shorter than its diff:
```python
import functools

import jax
import jax.numpy as jnp
from jax import lax
from jax.experimental import pallas as pl
from jax.experimental.pallas import tpu as pltpu
from jax.sharding import PartitionSpec as P

ITERS = 3
MESH = pl.DeviceIdType.MESH
F32, BF16, I32 = jnp.float32, jnp.bfloat16, jnp.int32


def iota(shape, axis):
    return lax.broadcasted_iota(I32, shape, axis)


def thirds(x):
    high = x.astype(BF16).astype(F32)
    rest = x - high
    mid = rest.astype(BF16).astype(F32)
    return high, mid, rest - mid


def dot(a, b):
    return jnp.dot(a.astype(BF16), b.astype(BF16), preferred_element_type=F32)


def dot_nt(a, b):
    dims = (((1,), (1,)), ((), ()))
    return lax.dot_general(a.astype(BF16), b.astype(BF16), dims, preferred_element_type=F32)


def pick(selector, x):
    high, mid, low = thirds(x)
    return (dot(selector, low) + dot(selector, mid)) + dot(selector, high)


def kernel(
    dims,
    path_count, cluster_size, inc_path, inc_edge, partner,
    flow_start, demand, utility, incidence, capacity, dual_start,
    flows_out, duals_out,
    inc_f32, inc, slot_edge, slot_edge_t, choose, choose_t,
    ask_send, ask_recv, flow_send, flow_recv, sum_send, sum_recv,
    edge_send, edge_recv, border_send, border_recv,
    load_sem, send_sem, ask_sem, flow_sem, sum_sem, edge_sem, border_sem,
):
    clusters, shards, blocks, paths, incs, edges, slots, norm_bound, unit = dims
    step_size = 1.0 / (2.0 * norm_bound)
    cluster, shard = lax.axis_index("cluster"), lax.axis_index("shard")
    interior = edges - slots

    load = pltpu.make_async_copy(incidence, inc_f32, load_sem)
    load.start()

    barrier = pltpu.get_barrier_semaphore()

    def greet_shard(k, _):
        pl.semaphore_signal(barrier, inc=1, device_id=(cluster, lax.rem(shard + k, shards)), device_id_type=MESH)
        return 0

    def greet_cluster(k, _):
        pl.semaphore_signal(barrier, inc=1, device_id=(lax.rem(cluster + k, clusters), shard), device_id_type=MESH)
        return 0

    lax.fori_loop(1, shards, greet_shard, 0)
    lax.fori_loop(1, clusters, greet_cluster, 0)
    pl.semaphore_wait(barrier, shards + clusters - 2)

    def to_shards(src, dst, sem):
        def one(k, _):
            peer = lax.rem(shard + k, shards)
            pltpu.make_async_remote_copy(
                src_ref=src.at[peer], dst_ref=dst.at[shard], send_sem=send_sem.at[sem[1]], recv_sem=sem[0],
                device_id=(cluster, peer), device_id_type=MESH).start()
            return 0
        lax.fori_loop(1, shards, one, 0)
        dst[shard] = src[shard]

    def to_clusters(src, dst, sem):
        def one(k, _):
            peer = lax.rem(cluster + k, clusters)
            pltpu.make_async_remote_copy(
                src_ref=src, dst_ref=dst.at[cluster], send_sem=send_sem.at[sem[1]], recv_sem=sem[0],
                device_id=(peer, shard), device_id_type=MESH).start()
            return 0
        lax.fori_loop(1, clusters, one, 0)
        dst[cluster] = src[...]

    def wait(dst, sem, count):
        whole = pltpu.make_async_remote_copy(
            src_ref=dst.at[pl.ds(0, count)], dst_ref=dst.at[pl.ds(0, count)], send_sem=send_sem.at[sem[1]],
            recv_sem=sem[0], device_id=(cluster, lax.rem(shard + 1, shards)), device_id_type=MESH)
        whole.wait_recv()
        whole.wait_send()

    ask, flow, total, edge = (ask_sem, 0), (flow_sem, 1), (sum_sem, 2), (edge_sem, 3)

    def border_first(ref):
        x = ref[...]
        return jnp.concatenate([x[interior:], jnp.zeros((8 - edges, x.shape[1]), F32), x[:interior]], axis=0)

    cap = border_first(capacity)
    dual = border_first(dual_start)
    edge_send[...] = jnp.concatenate([cap[:4], dual[:4]], axis=0)
    to_clusters(edge_send, edge_recv, edge)

    rows, lanes = iota((128, 128), 0), iota((128, 128), 1)
    row_dev, row_slot, row_half = rows >> 2, (rows >> 1) & 1, rows & 1
    lane1 = iota((1, 128), 1)
    lane_path = jnp.full((1, 128), -1, I32)
    for i in range(incs):
        lane_path = jnp.where(lane1 == i, inc_path[i], lane_path)
    owner = (lane_path >> 4) == row_dev
    before = dot(owner.astype(F32), (rows < lanes).astype(F32))
    slot = owner & (before == row_slot.astype(F32))
    wanted = jnp.sum(jnp.where(slot, (lane_path & 15) + 1, 0).astype(F32), axis=1, keepdims=True) - 1.0
    ask_send[...] = jnp.broadcast_to(wanted, (128, 128)).reshape(ask_send.shape)
    to_shards(ask_send, ask_recv, ask)

    lane_q = iota((1, 512), 1)
    lane_edge = jnp.full((1, 512), -1, I32)
    for i in range(incs):
        lane_edge = jnp.where((lane_q >> 4) == i, (inc_edge[i] + (8 - interior)) & 7, lane_edge)
    spread = (iota((128, 512), 0) == (iota((128, 512), 1) >> 4)).astype(F32)
    fits = (lane_edge == (lane_q & 7)) & (((lane_q >> 3) & 1) == (iota((128, 512), 0) & 1))
    both = jnp.where(fits, dot(slot.astype(F32), spread), 0.0)
    slot_edge[...] = both.astype(BF16)
    slot_edge_t[...] = both.T.astype(BF16)

    def halves(ref):
        x = ref[...]
        return jnp.concatenate([x[:, :128], x[:, 128:]], axis=0)

    low_flow, top_flow, gain = halves(flow_start), halves(demand), halves(utility)
    row32 = iota((32, 128), 0)
    count = jnp.zeros((32, 128), I32)
    for b in range(blocks):
        count = jnp.where((row32 & 15) == b, path_count[b], count)
    live = (((row32 & 15) < cluster_size[0]) & ((row32 >> 4) * 128 + iota((32, 128), 1) < count)).astype(F32)
    flows = jnp.minimum(jnp.maximum(low_flow, 0.0), top_flow) * live

    load.wait()

    def shrink(i, _):
        inc[pl.ds(pl.multiple_of(i * paths, paths), paths), :] = inc_f32[i].astype(BF16)
        return 0
    lax.fori_loop(0, incs, shrink, 0)

    partner_row = jnp.full((4, 128), -1, I32)
    for k in range(slots):
        partner_row = jnp.where(iota((4, 128), 0) == k, partner[0, k], partner_row)
    partner8 = jnp.concatenate([partner_row, partner_row], axis=0)
    wait(edge_recv, edge, clusters - 1)
    twin = jnp.zeros((8, 128), F32)
    for c in range(clusters):
        twin = twin + jnp.where(partner8 == c, edge_recv[c], 0.0)
    limit = unit * jnp.concatenate([0.5 * (cap[:4] + twin[:4]), cap[4:]], axis=0)
    duals = jnp.concatenate([0.5 * (dual[:4] + twin[4:]), dual[4:]], axis=0)

    wait(ask_recv, ask, shards - 1)
    asked = ask_recv[...].reshape(128, 128)
    chosen = ((asked == (lanes & 15).astype(F32)) & ((lanes >> 4) == row_half)).astype(F32)
    choose[...] = chosen.astype(BF16)
    choose_t[...] = chosen.T.astype(BF16)

    def share(flows):
        flow_send[...] = pick(choose[:, :32], flows).reshape(flow_send.shape)
        to_shards(flow_send, flow_recv, flow)

    def total_load(t):
        wait(flow_recv, flow, shards - 1)
        got = flow_recv[...].reshape(128, 128)
        parts = dot(slot_edge_t[...], jnp.concatenate(thirds(got), axis=1))
        columns = []
        for q in range(2 * incs):
            chunk = parts[q * 8:q * 8 + 8]
            columns.append(jnp.concatenate([chunk[:, :128], chunk[:, 128:256], chunk[:, 256:]], axis=0).astype(BF16))
        sums = dot(jnp.concatenate(columns, axis=1), inc[...])
        own = (sums[16:] + sums[8:16]) + sums[:8]
        border_send[...] = own[:4]
        border = (border_sem.at[t], 4)
        to_clusters(border_send, border_recv.at[t], border)
        wait(border_recv.at[t], border, clusters - 1)
        twin = jnp.zeros((4, 128), F32)
        for c in range(clusters):
            twin = twin + jnp.where(partner_row == c, border_recv[t, c], 0.0)
        return jnp.concatenate([own[:4] + twin, own[4:]], axis=0)

    def settle(load, duals):
        split = jnp.minimum(limit, load + duals)
        duals = (duals + load) - split
        return (load - split) + duals, duals

    share(flows)
    residual, duals = settle(total_load(0), duals)

    def iterate(t, carry):
        flows, residual, duals = carry
        parts = dot_nt(jnp.concatenate(thirds(residual), axis=0), inc[...])
        back = (parts[16:] + parts[8:16]) + parts[:8]
        back = jnp.concatenate([back[:, q * 128:q * 128 + 128] for q in range(2 * incs)], axis=0)
        sum_send[...] = pick(slot_edge[...], back).reshape(sum_send.shape)
        to_shards(sum_send, sum_recv, total)
        wait(sum_recv, total, shards - 1)
        grad = pick(choose_t[:32, :], sum_recv[...].reshape(128, 128))
        flows = jnp.minimum(jnp.maximum(flows - step_size * (grad - gain), 0.0), top_flow) * live
        share(flows)
        residual, duals = settle(total_load(t), duals)
        return flows, residual, duals

    flows, residual, duals = lax.fori_loop(1, ITERS + 1, iterate, (flows, residual, duals))
    flows_out[...] = jnp.concatenate([flows[:16], flows[16:]], axis=1)
    duals_out[...] = jnp.concatenate([duals[4:], duals[:slots]], axis=0)


def body(flow_start, demand, utility, path_count, cluster_size, incidence, inc_path, inc_edge, capacity, dual_start, partner):
    blocks, paths = flow_start.shape
    incs, _, width = incidence.shape
    edges, slots = capacity.shape[0], partner.shape[1]
    clusters, shards = lax.axis_size("cluster"), lax.axis_size("shard")
    norm_bound = max(2, incs * incs * paths * width // (1024 * edges * blocks))
    unit = float(max(1, incs * paths // (160 * edges)))
    dims = (clusters, shards, blocks, paths, incs, edges, slots, norm_bound, unit)
    smem, vmem, hbm = (pl.BlockSpec(memory_space=m) for m in (pltpu.SMEM, pltpu.VMEM, pl.ANY))
    dma = pltpu.SemaphoreType.DMA
    message = pltpu.VMEM((shards, 4, 128), F32)
    return pl.pallas_call(
        functools.partial(kernel, dims),
        out_shape=(jax.ShapeDtypeStruct(flow_start.shape, F32), jax.ShapeDtypeStruct(capacity.shape, F32)),
        in_specs=[smem] * 5 + [vmem, vmem, vmem, hbm, vmem, vmem],
        out_specs=(vmem, vmem),
        scratch_shapes=[
            pltpu.VMEM((incs, paths, width), F32),
            pltpu.VMEM((incs * paths, width), BF16),
            pltpu.VMEM((128, 512), BF16),
            pltpu.VMEM((512, 128), BF16),
            pltpu.VMEM((128, 128), BF16),
            pltpu.VMEM((128, 128), BF16),
            message, message, message, message, message, message,
            pltpu.VMEM((8, 128), F32),
            pltpu.VMEM((clusters, 8, 128), F32),
            pltpu.VMEM((4, 128), F32),
            pltpu.VMEM((ITERS + 1, clusters, 4, 128), F32),
            dma(()), dma((5,)), dma(()), dma(()), dma(()), dma(()), dma((ITERS + 1,)),
        ],
        compiler_params=pltpu.CompilerParams(
            collective_id=0, has_side_effects=True, vmem_limit_bytes=40 * 1024 * 1024),
    )(path_count, cluster_size, inc_path, inc_edge, partner, flow_start, demand, utility, incidence, capacity, dual_start)


def solution(mesh):
    both = P(("cluster", "shard"))
    rows = P(("cluster", "shard"), None)
    return jax.shard_map(
        body,
        mesh=mesh,
        in_specs=(rows, rows, rows, both, P("cluster"), P(("cluster", "shard"), None, None), both, both, rows, rows, P("cluster", None)),
        out_specs=(rows, rows),
        check_vma=False,
    )
```

time: 921 us -> 89.9 us (0.10)
  waiting for transfers between devices: 419 us -> 0 us
  blocking collectives: 268 us -> 0 us
  starting transfers between devices: 165 us -> 0 us
  Pallas kernels: 0 us -> 78.6 us
  matrix products: 43 us -> 0 us
  between operations: 14.6 us -> 1.31 us
    reduce_scatter x3 -> x0, waiting for transfers between devices: 385 us -> none  [body(): lax.psum_scatter(jnp.dot(rows_pick, terms, precision=exact_mode), 'shard'...]
    all_gather x4 -> x0, blocking collectives: 268 us -> none  [shared_flows(): return lax.all_gather(flows_now, 'shard', axis=0, tiled=True)]
    all_to_all x5 -> x0, starting transfers between devices: 165 us -> none  [the longest x4 161 us: twin_of(): lax.all_to_all(outgoing, 'cluster', split_axis=0, concat_axis=0, tiled=True)]
    pallas_call x0 -> x1, Pallas kernels: none -> 78.6 us  [body(): pl.pallas_call(functools.partial(kernel, dims), out_shape=(jax.ShapeDtype...]
    dot_general x24 -> x0, matrix products: 43 us -> none  [the longest x4 17.3 us: load_of_rows(): terms = jnp.einsum('ipe,ip->ie', incidence, picked, precision=exact_mode)]
    all_to_all x5 -> x0, waiting for transfers between devices: 33.5 us -> none  [the longest x4 26.7 us: twin_of(): lax.all_to_all(outgoing, 'cluster', split_axis=0, concat_axis=0, tiled=True)]
    unnamed x20 -> x22, local copies, waits for them, and re-layouts: 0.04 us -> 9.52 us
  transfers between devices with their start and end apart: 8 -> 0, of which waited for: 8 -> 0; matrix products, arithmetic and copies ran while one was open for 0% -> 0% of each run, Pallas kernels for 0% -> 0%
where the time goes in v1:
time: 89.9 us; the launch traced here: 89.4 us
  Pallas kernels  78.6 us (87%)
  local copies, waits for them, and re-layouts  9.52 us (11%)
  between operations  1.31 us (1%)
    pallas_call x1, Pallas kernels, body(): pl.pallas_call(functools.partial(kernel, dims), out_shape=(jax.ShapeDtype...  78.6 us
    unnamed x22, local copies, waits for them, and re-layouts  9.52 us

profile of v1, /device:TPU:1, one launch (start us, length us, event | category | flops | bytes accessed | tf_op | source)
XLA Modules:
  0.0 89.4 jit_solution(2786765142048869865)
XLA Ops:
  1.3 0.0 copy-start
  1.3 2.2 %copy-done = f32[32,256,128]{2,1,0:T(8,128)S(1)} copy-done((f32[32,256,128]{2,1,0:T(8,128)S(1)}, f32[32,256,128]{2,1,0:T(8,128)}, u32[]{:S(2)}) %copy-start) | copy-done | bytes 4194328
  3.5 0.0 copy-start.1
  3.5 0.7 copy-done.1
  4.2 0.0 copy-start.2
  4.2 0.7 copy-done.2
  4.9 0.0 copy-start.3
  4.9 0.7 copy-done.3
  5.6 0.0 copy-start.4
  5.6 0.7 copy-done.4
  6.3 0.0 copy-start.5
  6.3 0.7 copy-done.5
  7.0 0.0 copy-start.6
  7.0 0.7 copy-done.6
  7.7 0.0 copy-start.7
  7.7 0.7 copy-done.7
  8.3 0.0 copy-start.8
  8.3 0.7 copy-done.8
  9.0 0.0 copy-start.9
  9.0 0.7 copy-done.9
  9.6 78.6 %shard_map.122 = (f32[16,256]{1,0:T(8,128)S(1)}, f32[7,128]{1,0:T(8,128)S(1)}) custom-call(s32[16]{0:T(128)S(1)} %copy-done.6, s32[1]{0:T(128)S(6)} %copy.15.cluster_size, s32[32]{0:T(128)S(1)} %copy-done.7, s32[32]{0:T(128)S(1)} %copy-done.8, s32[1,3]{1,0:T(1,128)S(1)} %copy-done.9, f32[16,256]{1,0:T(8,128)S(1)} %copy-done.1, f32[16,256]{1,0:T(8,128)S(1)} %copy-done.2, ...), custom_call_target="tpu_custom_call" | custom-call | tf_op jit(solution)/shard_map/pallas_call | solution.py:230
  88.2 0.6 copy.16
  88.8 0.6 copy.17
Async XLA Ops:
  1.3 2.2 %copy-start = (f32[32,256,128]{2,1,0:T(8,128)S(1)}, f32[32,256,128]{2,1,0:T(8,128)}, u32[]{:S(2)}) copy-start(f32[32,256,128]{2,1,0:T(8,128)} %incidence.1) | copy-start | bytes 12582916
  3.5 0.7 copy-start.1
  4.2 0.7 copy-start.2
  4.9 0.7 copy-start.3
  5.6 0.7 copy-start.4
  6.3 0.7 copy-start.5
  7.0 0.7 copy-start.6
  7.7 0.7 copy-start.7
  8.3 0.7 copy-start.8
  9.0 0.7 copy-start.9

commit v2 on v1

v2 whole, which is shorter than its diff:
```python
import functools

import jax
import jax.numpy as jnp
from jax import lax
from jax.experimental import pallas as pl
from jax.experimental.pallas import tpu as pltpu
from jax.sharding import PartitionSpec as P

ITERS = 3
GRID = (4, 2, 4)
MESH = pl.DeviceIdType.MESH
F32, BF16, I32 = jnp.float32, jnp.bfloat16, jnp.int32


def iota(shape, axis):
    return lax.broadcasted_iota(I32, shape, axis)


def thirds(x):
    high = x.astype(BF16).astype(F32)
    rest = x - high
    mid = rest.astype(BF16).astype(F32)
    return high, mid, rest - mid


def dot(a, b):
    return jnp.dot(a.astype(BF16), b.astype(BF16), preferred_element_type=F32)


def dot_nt(a, b):
    dims = (((1,), (1,)), ((), ()))
    return lax.dot_general(a.astype(BF16), b.astype(BF16), dims, preferred_element_type=F32)


def pick(selector, x):
    high, mid, low = thirds(x)
    return (dot(selector, low) + dot(selector, mid)) + dot(selector, high)


def hops(offset):
    return sum(min(d, n - d) for d, n in zip(offset, GRID))


NEAR = sorted(((x, z, y) for x in range(4) for z in range(2) for y in range(4) if hops((x, z, y)) <= 2), key=hops)
BACK = [NEAR.index(tuple(-d % n for d, n in zip(offset, GRID))) for offset in NEAR]
FAR_FIRST = sorted(range(1, 32), key=lambda u: -(hops(NEAR[u]) if u < 16 else 5 - hops(NEAR[u - 16])))
NEAR_FAR_FIRST = [u for u in FAR_FIRST if u < 16]


def kernel(
    dims,
    path_count_hbm, cluster_size_hbm, inc_path_hbm, inc_edge_hbm, partner_hbm,
    flow_start_hbm, demand_hbm, utility_hbm, incidence_hbm, capacity_hbm, dual_start_hbm,
    flows_out, duals_out,
    path_count, cluster_size, inc_path, inc_edge, partner,
    flow_start, demand, utility, incidence, capacity, dual_start,
    inc, slot_edge, slot_edge_t, choose, choose_t,
    ask_send, ask_recv, flow_send, flow_recv, sum_send, sum_recv,
    edge_send, edge_recv, border_send, border_recv, start_send, start_recv, rest_send, rest_recv,
    load_sem, send_sem, ask_sem, flow_sem, sum_sem, edge_sem, border_sem, start_sem, rest_sem,
):
    clusters, shards, blocks, paths, incs, edges, slots, norm_bound, unit = dims
    step_size = 1.0 / (2.0 * norm_bound)
    cluster, shard = lax.axis_index("cluster"), lax.axis_index("shard")
    interior = edges - slots

    barrier = pltpu.get_barrier_semaphore()

    def greet_shard(k, _):
        pl.semaphore_signal(barrier, inc=1, device_id=(cluster, lax.rem(shard + k, shards)), device_id_type=MESH)
        return 0

    def greet_cluster(k, _):
        pl.semaphore_signal(barrier, inc=1, device_id=(lax.rem(cluster + k, clusters), shard), device_id_type=MESH)
        return 0

    lax.fori_loop(1, shards, greet_shard, 0)
    lax.fori_loop(1, clusters, greet_cluster, 0)

    loads = [
        pltpu.make_async_copy(src, dst, load_sem.at[n])
        for n, (src, dst) in enumerate((
            (inc_path_hbm, inc_path), (capacity_hbm, capacity), (dual_start_hbm, dual_start),
            (path_count_hbm, path_count), (cluster_size_hbm, cluster_size), (flow_start_hbm, flow_start),
            (demand_hbm, demand), (utility_hbm, utility), (inc_edge_hbm, inc_edge), (partner_hbm, partner),
            (incidence_hbm, incidence)))]
    for copy in loads:
        copy.start()

    at_x = [lax.rem(shard // 8 + d, 4) * 8 for d in range(4)]
    at_z = [lax.rem(shard // 4 + d, 2) * 4 for d in range(2)]
    at_y = [lax.rem(shard + d, 4) for d in range(4)]
    near = [at_x[x] + at_z[z] + at_y[y] for x, z, y in NEAR]

    def other_end(index):
        return lax.rem(index // 8 + 2, 4) * 8 + lax.rem(index // 4 + 1, 2) * 4 + lax.rem(index + 2, 4)

    far = [other_end(index) for index in near]

    def send(src, dst, send_to, recv_to, peer):
        pltpu.make_async_remote_copy(
            src_ref=src, dst_ref=dst, send_sem=send_to, recv_sem=recv_to,
            device_id=(cluster, peer), device_id_type=MESH).start()

    def to_all(src, dst, send_to, recv_to):
        for u in FAR_FIRST:
            peer, place = (near[u], BACK[u]) if u < 16 else (far[u - 16], 16 + BACK[u - 16])
            send(src.at[u], dst.at[place], send_to, recv_to, peer)

    def to_near(src, dst, send_to, recv_to):
        for u in NEAR_FAR_FIRST:
            send(src.at[u], dst.at[BACK[u]], send_to, recv_to, near[u])

    def to_clusters(src, dst, send_to, recv_to):
        for k in (4, 3, 5, 2, 6, 1, 7):
            pltpu.make_async_remote_copy(
                src_ref=src, dst_ref=dst.at[cluster], send_sem=send_to, recv_sem=recv_to,
                device_id=(lax.rem(cluster + k, clusters), shard), device_id_type=MESH).start()
        dst[cluster] = src[...]

    def wait(dst, send_to, recv_to):
        whole = pltpu.make_async_remote_copy(
            src_ref=dst, dst_ref=dst, send_sem=send_to, recv_sem=recv_to,
            device_id=(cluster, far[0]), device_id_type=MESH)
        whole.wait_recv()
        whole.wait_send()

    tile_role = iota((8, 128), 0) >> 2
    rows, lanes = iota((128, 128), 0), iota((128, 128), 1)
    row_slot, row_half = (rows >> 1) & 1, rows & 1
    row_dev = jnp.concatenate([jnp.where(tile_role == 0, near[q], far[q]) for q in range(16)], axis=0)
    lane1 = iota((1, 128), 1)
    loads[0].wait()
    lane_path = jnp.full((1, 128), -1, I32)
    for i in range(incs):
        lane_path = jnp.where(lane1 == i, inc_path[i], lane_path)
    owner = (lane_path >> 4) == row_dev
    before = dot(owner.astype(F32), (rows < lanes).astype(F32))
    slot = owner & (before == row_slot.astype(F32))

    def fill(dst, x):
        for q in range(16):
            tile = x[q * 8:q * 8 + 8]
            dst[q] = tile
            dst[16 + q] = pltpu.roll(tile, 4, 0)

    wanted = jnp.sum(jnp.where(slot, (lane_path & 15) + 1, 0).astype(F32), axis=1, keepdims=True) - 1.0
    fill(ask_send, jnp.broadcast_to(wanted, (128, 128)))

    def border_first(ref):
        x = ref[...]
        return jnp.concatenate([x[interior:], jnp.zeros((8 - edges, x.shape[1]), F32), x[:interior]], axis=0)

    loads[1].wait()
    loads[2].wait()
    cap = border_first(capacity)
    dual = border_first(dual_start)
    edge_send[...] = jnp.concatenate([cap[:4], dual[:4]], axis=0)

    def halves(ref):
        x = ref[...]
        return jnp.concatenate([x[:, :128], x[:, 128:]], axis=0)

    for copy in loads[3:8]:
        copy.wait()
    row32 = iota((32, 128), 0)
    count = jnp.zeros((32, 128), I32)
    for b in range(blocks):
        count = jnp.where((row32 & 15) == b, path_count[b], count)
    live = (((row32 & 15) < cluster_size[0]) & ((row32 >> 4) * 128 + iota((32, 128), 1) < count)).astype(F32)
    top = halves(demand) * live
    start = jnp.minimum(jnp.maximum(halves(flow_start), 0.0), top)
    gain = halves(utility)
    start_send[...] = start
    rest_send[0] = top
    rest_send[1] = gain

    pl.semaphore_wait(barrier, shards + clusters - 2)
    send(start_send, start_recv, send_sem.at[4], start_sem, far[0])
    to_all(ask_send, ask_recv, send_sem.at[0], ask_sem)
    ask_recv[0] = ask_send[0]
    to_clusters(edge_send, edge_recv, send_sem.at[1], edge_sem)
    send(rest_send, rest_recv, send_sem.at[5], rest_sem, far[0])

    loads[8].wait()
    lane_q = iota((1, 512), 1)
    lane_edge = jnp.full((1, 512), -1, I32)
    for i in range(incs):
        lane_edge = jnp.where((lane_q >> 4) == i, (inc_edge[i] + (8 - interior)) & 7, lane_edge)
    spread = (iota((128, 512), 0) == (iota((128, 512), 1) >> 4)).astype(F32)
    fits = (lane_edge == (lane_q & 7)) & (((lane_q >> 3) & 1) == (iota((128, 512), 0) & 1))
    both = jnp.where(fits, dot(slot.astype(F32), spread), 0.0)
    slot_edge[...] = both.astype(BF16)
    slot_edge_t[...] = both.T.astype(BF16)

    loads[9].wait()
    partner_row = jnp.full((4, 128), -1, I32)
    for k in range(slots):
        partner_row = jnp.where(iota((4, 128), 0) == k, partner[0, k], partner_row)
    partner8 = jnp.concatenate([partner_row, partner_row], axis=0)

    loads[10].wait()

    def shrink(i, _):
        inc[pl.ds(pl.multiple_of(i * paths, paths), paths), :] = incidence[i].astype(BF16)
        return 0
    lax.fori_loop(0, incs, shrink, 0)

    wait(ask_recv.at[pl.ds(0, shards - 1)], send_sem.at[0], ask_sem)
    asked = ask_recv[...].reshape(256, 128)
    rows2, lanes2 = iota((256, 128), 0), iota((256, 128), 1)
    chosen = ((asked == (lanes2 & 15).astype(F32)) & (((lanes2 >> 4) & 1) == (rows2 & 1))
              & ((lanes2 >> 5) == ((rows2 >> 2) & 1))).astype(F32)
    choose[...] = chosen[:128].astype(BF16)
    choose_t[...] = chosen.T.astype(BF16)

    def share(flows):
        x = pick(choose[:, :64], flows)
        for q in range(16):
            flow_send[q] = x[q * 8:q * 8 + 8]
        to_near(flow_send, flow_recv, send_sem.at[2], flow_sem)
        flow_recv[0] = flow_send[0]

    def total_load(t):
        wait(flow_recv.at[pl.ds(0, 15)], send_sem.at[2], flow_sem)
        got = flow_recv[...].reshape(128, 128)
        parts = dot(slot_edge_t[...], jnp.concatenate(thirds(got), axis=1))
        columns = []
        for q in range(2 * incs):
            chunk = parts[q * 8:q * 8 + 8]
            columns.append(jnp.concatenate([chunk[:, :128], chunk[:, 128:256], chunk[:, 256:]], axis=0).astype(BF16))
        sums = dot(jnp.concatenate(columns, axis=1), inc[...])
        own = (sums[16:] + sums[8:16]) + sums[:8]
        border_send[...] = own[:4]
        to_clusters(border_send, border_recv.at[t], send_sem.at[3], border_sem.at[t])
        wait(border_recv.at[t, pl.ds(0, clusters - 1)], send_sem.at[3], border_sem.at[t])
        twin = jnp.zeros((4, 128), F32)
        for c in range(clusters):
            twin = twin + jnp.where(partner_row == c, border_recv[t, c], 0.0)
        return jnp.concatenate([own[:4] + twin, own[4:]], axis=0)

    def settle(load, duals):
        split = jnp.minimum(limit, load + duals)
        duals = (duals + load) - split
        return (load - split) + duals, duals

    wait(start_recv, send_sem.at[4], start_sem)
    flows = jnp.concatenate([start, start_recv[...]], axis=0)
    share(flows)

    wait(rest_recv, send_sem.at[5], rest_sem)
    top = jnp.concatenate([top, rest_recv[0]], axis=0)
    gain = jnp.concatenate([gain, rest_recv[1]], axis=0)
    wait(edge_recv.at[pl.ds(0, clusters - 1)], send_sem.at[1], edge_sem)
    twin = jnp.zeros((8, 128), F32)
    for c in range(clusters):
        twin = twin + jnp.where(partner8 == c, edge_recv[c], 0.0)
    limit = unit * jnp.concatenate([0.5 * (cap[:4] + twin[:4]), cap[4:]], axis=0)
    duals = jnp.concatenate([0.5 * (dual[:4] + twin[4:]), dual[4:]], axis=0)

    residual, duals = settle(total_load(0), duals)

    def iterate(t, carry):
        flows, residual, duals = carry
        turn = lax.rem(t, 2)
        parts = dot_nt(jnp.concatenate(thirds(residual), axis=0), inc[...])
        back = (parts[16:] + parts[8:16]) + parts[:8]
        back = jnp.concatenate([back[:, q * 128:q * 128 + 128] for q in range(2 * incs)], axis=0)
        fill(sum_send, pick(slot_edge[...], back))
        to_all(sum_send, sum_recv.at[turn], send_sem.at[0], sum_sem.at[turn])
        sum_recv[turn, 0] = sum_send[0]
        wait(sum_recv.at[turn, pl.ds(0, shards - 1)], send_sem.at[0], sum_sem.at[turn])
        grad = pick(choose_t[:64, :], sum_recv[turn].reshape(256, 128))
        flows = jnp.minimum(jnp.maximum(flows - step_size * (grad - gain), 0.0), top)
        share(flows)
        residual, duals = settle(total_load(t), duals)
        return flows, residual, duals

    flows, residual, duals = lax.fori_loop(1, ITERS + 1, iterate, (flows, residual, duals))
    flows_out[...] = jnp.concatenate([flows[:16], flows[16:32]], axis=1)
    duals_out[...] = jnp.concatenate([duals[4:], duals[:slots]], axis=0)


def body(flow_start, demand, utility, path_count, cluster_size, incidence, inc_path, inc_edge, capacity, dual_start, partner):
    blocks, paths = flow_start.shape
    incs, _, width = incidence.shape
    edges, slots = capacity.shape[0], partner.shape[1]
    clusters, shards = lax.axis_size("cluster"), lax.axis_size("shard")
    norm_bound = max(2, incs * incs * paths * width // (1024 * edges * blocks))
    unit = float(max(1, incs * paths // (160 * edges)))
    dims = (clusters, shards, blocks, paths, incs, edges, slots, norm_bound, unit)
    scalars = (path_count, cluster_size, inc_path, inc_edge, partner)
    arrays = (flow_start, demand, utility, incidence, capacity, dual_start)
    dma = pltpu.SemaphoreType.DMA
    message = pltpu.VMEM((shards, 8, 128), F32)
    near = pltpu.VMEM((16, 8, 128), F32)
    return pl.pallas_call(
        functools.partial(kernel, dims),
        out_shape=(jax.ShapeDtypeStruct(flow_start.shape, F32), jax.ShapeDtypeStruct(capacity.shape, F32)),
        in_specs=[pl.BlockSpec(memory_space=pltpu.HBM)] * (len(scalars) + len(arrays)),
        out_specs=[pl.BlockSpec(memory_space=pltpu.VMEM)] * 2,
        scratch_shapes=[pltpu.SMEM(x.shape, I32) for x in scalars] + [pltpu.VMEM(x.shape, F32) for x in arrays] + [
            pltpu.VMEM((incs * paths, width), BF16),
            pltpu.VMEM((128, 512), BF16),
            pltpu.VMEM((512, 128), BF16),
            pltpu.VMEM((128, 128), BF16),
            pltpu.VMEM((128, 256), BF16),
            message, message, near, near, message, pltpu.VMEM((2, shards, 8, 128), F32),
            pltpu.VMEM((8, 128), F32),
            pltpu.VMEM((clusters, 8, 128), F32),
            pltpu.VMEM((4, 128), F32),
            pltpu.VMEM((ITERS + 1, clusters, 4, 128), F32),
            pltpu.VMEM((32, 128), F32), pltpu.VMEM((32, 128), F32),
            pltpu.VMEM((2, 32, 128), F32), pltpu.VMEM((2, 32, 128), F32),
            dma((11,)), dma((6,)), dma(()), dma(()), dma((2,)), dma(()), dma((ITERS + 1,)), dma(()), dma(()),
        ],
        compiler_params=pltpu.CompilerParams(
            collective_id=0, has_side_effects=True, vmem_limit_bytes=40 * 1024 * 1024),
    )(*scalars, *arrays)


def solution(mesh):
    both = P(("cluster", "shard"))
    rows = P(("cluster", "shard"), None)
    return jax.shard_map(
        body,
        mesh=mesh,
        in_specs=(rows, rows, rows, both, P("cluster"), P(("cluster", "shard"), None, None), both, both, rows, rows, P("cluster", None)),
        out_specs=(rows, rows),
        check_vma=False,
    )
```

time: 89.9 us -> 85.9 us (0.956)
  Pallas kernels: 78.6 us -> 74.6 us
    pallas_call x1, Pallas kernels: 78.6 us -> 74.6 us  [body(): pl.pallas_call(functools.partial(kernel, dims), out_shape=(jax.ShapeDtype...]
where the time goes in v2:
time: 85.9 us; the launch traced here: 85.4 us
  Pallas kernels  74.6 us (87%)
  local copies, waits for them, and re-layouts  9.52 us (11%)
  between operations  1.31 us (2%)
    pallas_call x1, Pallas kernels, body(): pl.pallas_call(functools.partial(kernel, dims), out_shape=(jax.ShapeDtype...  74.6 us
    unnamed x22, local copies, waits for them, and re-layouts  9.52 us

profile of v2, /device:TPU:1, one launch (start us, length us, event | category | flops | bytes accessed | tf_op | source)
XLA Modules:
  0.0 85.4 jit_solution(3265651691421999909)
XLA Ops:
  1.3 0.0 copy-start
  1.3 2.2 %copy-done = f32[32,256,128]{2,1,0:T(8,128)S(1)} copy-done((f32[32,256,128]{2,1,0:T(8,128)S(1)}, f32[32,256,128]{2,1,0:T(8,128)}, u32[]{:S(2)}) %copy-start) | copy-done | bytes 4194328
  3.5 0.0 copy-start.1
  3.5 0.7 copy-done.1
  4.2 0.0 copy-start.2
  4.2 0.7 copy-done.2
  4.9 0.0 copy-start.3
  4.9 0.7 copy-done.3
  5.6 0.0 copy-start.4
  5.6 0.7 copy-done.4
  6.3 0.0 copy-start.5
  6.3 0.7 copy-done.5
  7.0 0.0 copy-start.6
  7.0 0.7 copy-done.6
  7.7 0.0 copy-start.7
  7.7 0.7 copy-done.7
  8.3 0.0 copy-start.8
  8.3 0.7 copy-done.8
  9.0 0.0 copy-start.9
  9.0 0.7 copy-done.9
  9.6 74.6 %shard_map.122 = (f32[16,256]{1,0:T(8,128)S(1)}, f32[7,128]{1,0:T(8,128)S(1)}) custom-call(s32[16]{0:T(128)S(1)} %copy-done.6, s32[1]{0:T(128)S(6)} %copy.15.cluster_size_hbm, s32[32]{0:T(128)S(1)} %copy-done.7, s32[32]{0:T(128)S(1)} %copy-done.8, s32[1,3]{1,0:T(1,128)S(1)} %copy-done.9, f32[16,256]{1,0:T(8,128)S(1)} %copy-done.1, f32[16,256]{1,0:T(8,128)S(1)} %copy-done.2, ...), custom_call_target="tpu_custom_call" | custom-call | tf_op jit(solution)/shard_map/pallas_call | solution.py:298
  84.2 0.6 copy.16
  84.8 0.6 copy.17
Async XLA Ops:
  1.3 2.2 %copy-start = (f32[32,256,128]{2,1,0:T(8,128)S(1)}, f32[32,256,128]{2,1,0:T(8,128)}, u32[]{:S(2)}) copy-start(f32[32,256,128]{2,1,0:T(8,128)} %incidence_hbm.1) | copy-start | bytes 12582916
  3.5 0.7 copy-start.1
  4.2 0.7 copy-start.2
  4.9 0.7 copy-start.3
  5.6 0.7 copy-start.4
  6.3 0.7 copy-start.5
  7.0 0.7 copy-start.6
  7.7 0.7 copy-start.7
  8.3 0.7 copy-start.8
  9.0 0.7 copy-start.9

commit v3 on v2

--- a/solution.py
+++ b/solution.py
@@ -316,7 +316,7 @@
             dma((11,)), dma((6,)), dma(()), dma(()), dma((2,)), dma(()), dma((ITERS + 1,)), dma(()), dma(()),
         ],
         compiler_params=pltpu.CompilerParams(
-            collective_id=0, has_side_effects=True, vmem_limit_bytes=40 * 1024 * 1024),
+            collective_id=0, has_side_effects=True, vmem_limit_bytes=60 * 1024 * 1024),
     )(*scalars, *arrays)
 
 

time: 85.9 us -> 79.7 us (0.928)
  local copies, waits for them, and re-layouts: 9.52 us -> 2.59 us
  Pallas kernels: 74.6 us -> 75.5 us
    unnamed x22 -> x2, local copies, waits for them, and re-layouts: 9.52 us -> 2.59 us
    pallas_call x1, Pallas kernels: 74.6 us -> 75.5 us  [body(): pl.pallas_call(functools.partial(kernel, dims), out_shape=(jax.ShapeDtype...]
where the time goes in v3:
time: 79.7 us; the launch traced here: 79.4 us
  Pallas kernels  75.5 us (95%)
  local copies, waits for them, and re-layouts  2.59 us (3%)
  between operations  1.29 us (2%)
    pallas_call x1, Pallas kernels, body(): pl.pallas_call(functools.partial(kernel, dims), out_shape=(jax.ShapeDtype...  75.5 us
    unnamed x2, local copies, waits for them, and re-layouts  2.59 us

profile of v3, /device:TPU:1, one launch (start us, length us, event | category | flops | bytes accessed | tf_op | source)
XLA Modules:
  0.0 79.4 jit_solution(3151258459703474467)
XLA Ops:
  1.3 75.5 %shard_map.122 = (f32[16,256]{1,0:T(8,128)}, f32[7,128]{1,0:T(8,128)}) custom-call(s32[16]{0:T(128)} %path_count_hbm.1, s32[1]{0:T(128)S(6)} %copy.15.cluster_size_hbm, s32[32]{0:T(128)} %inc_path_hbm.1, s32[32]{0:T(128)} %inc_edge_hbm.1, s32[1,3]{1,0:T(1,128)} %partner_hbm.1, f32[16,256]{1,0:T(8,128)} %flow_start_hbm.1, f32[16,256]{1,0:T(8,128)} %demand_hbm.1, ...), custom_call_target="tpu_custom_call" | custom-call | tf_op jit(solution)/shard_map/pallas_call | solution.py:298
  76.8 1.3 %copy.16 = f32[16,256]{1,0:T(8,128)} copy(f32[16,256]{1,0:T(8,128)} %get-tuple-element.4) | data formatting | bytes 32768
  78.2 1.3 %copy.17 = f32[7,128]{1,0:T(8,128)} copy(f32[7,128]{1,0:T(8,128)} %get-tuple-element.5) | data formatting | bytes 7168

commit v4 on v3

--- a/solution.py
+++ b/solution.py
@@ -28,11 +28,6 @@
     return jnp.dot(a.astype(BF16), b.astype(BF16), preferred_element_type=F32)
 
 
-def dot_nt(a, b):
-    dims = (((1,), (1,)), ((), ()))
-    return lax.dot_general(a.astype(BF16), b.astype(BF16), dims, preferred_element_type=F32)
-
-
 def pick(selector, x):
     high, mid, low = thirds(x)
     return (dot(selector, low) + dot(selector, mid)) + dot(selector, high)
@@ -50,12 +45,12 @@
 
 def kernel(
     dims,
-    path_count_hbm, cluster_size_hbm, inc_path_hbm, inc_edge_hbm, partner_hbm,
+    cluster_size, path_count_hbm, inc_path_hbm, inc_edge_hbm, partner_hbm,
     flow_start_hbm, demand_hbm, utility_hbm, incidence_hbm, capacity_hbm, dual_start_hbm,
     flows_out, duals_out,
-    path_count, cluster_size, inc_path, inc_edge, partner,
+    path_count, inc_path, inc_edge, partner,
     flow_start, demand, utility, incidence, capacity, dual_start,
-    inc, slot_edge, slot_edge_t, choose, choose_t,
+    inc, inc_t, slot_edge, slot_edge_t, choose, choose_t,
     ask_send, ask_recv, flow_send, flow_recv, sum_send, sum_recv,
     edge_send, edge_recv, border_send, border_recv, start_send, start_recv, rest_send, rest_recv,
     load_sem, send_sem, ask_sem, flow_sem, sum_sem, edge_sem, border_sem, start_sem, rest_sem,
@@ -82,7 +77,7 @@
         pltpu.make_async_copy(src, dst, load_sem.at[n])
         for n, (src, dst) in enumerate((
             (inc_path_hbm, inc_path), (capacity_hbm, capacity), (dual_start_hbm, dual_start),
-            (path_count_hbm, path_count), (cluster_size_hbm, cluster_size), (flow_start_hbm, flow_start),
+            (path_count_hbm, path_count), (flow_start_hbm, flow_start),
             (demand_hbm, demand), (utility_hbm, utility), (inc_edge_hbm, inc_edge), (partner_hbm, partner),
             (incidence_hbm, incidence)))]
     for copy in loads:
@@ -162,7 +157,7 @@
         x = ref[...]
         return jnp.concatenate([x[:, :128], x[:, 128:]], axis=0)
 
-    for copy in loads[3:8]:
+    for copy in loads[3:7]:
         copy.wait()
     row32 = iota((32, 128), 0)
     count = jnp.zeros((32, 128), I32)
@@ -183,7 +178,7 @@
     to_clusters(edge_send, edge_recv, send_sem.at[1], edge_sem)
     send(rest_send, rest_recv, send_sem.at[5], rest_sem, far[0])
 
-    loads[8].wait()
+    loads[7].wait()
     lane_q = iota((1, 512), 1)
     lane_edge = jnp.full((1, 512), -1, I32)
     for i in range(incs):
@@ -194,16 +189,19 @@
     slot_edge[...] = both.astype(BF16)
     slot_edge_t[...] = both.T.astype(BF16)
 
-    loads[9].wait()
+    loads[8].wait()
     partner_row = jnp.full((4, 128), -1, I32)
     for k in range(slots):
         partner_row = jnp.where(iota((4, 128), 0) == k, partner[0, k], partner_row)
     partner8 = jnp.concatenate([partner_row, partner_row], axis=0)
 
-    loads[10].wait()
+    loads[9].wait()
 
     def shrink(i, _):
-        inc[pl.ds(pl.multiple_of(i * paths, paths), paths), :] = incidence[i].astype(BF16)
+        at = pl.ds(pl.multiple_of(i * paths, paths), paths)
+        block = incidence[i].astype(BF16)
+        inc[at, :] = block
+        inc_t[:, at] = block.T
         return 0
     lax.fori_loop(0, incs, shrink, 0)
 
@@ -264,7 +262,7 @@
     def iterate(t, carry):
         flows, residual, duals = carry
         turn = lax.rem(t, 2)
-        parts = dot_nt(jnp.concatenate(thirds(residual), axis=0), inc[...])
+        parts = dot(jnp.concatenate(thirds(residual), axis=0), inc_t[...])
         back = (parts[16:] + parts[8:16]) + parts[:8]
         back = jnp.concatenate([back[:, q * 128:q * 128 + 128] for q in range(2 * incs)], axis=0)
         fill(sum_send, pick(slot_edge[...], back))
@@ -282,6 +280,14 @@
     duals_out[...] = jnp.concatenate([duals[4:], duals[:slots]], axis=0)
 
 
+def write_out(flows, duals, flows_out, duals_out, sems):
+    copies = [pltpu.make_async_copy(flows, flows_out, sems.at[0]), pltpu.make_async_copy(duals, duals_out, sems.at[1])]
+    for copy in copies:
+        copy.start()
+    for copy in copies:
+        copy.wait()
+
+
 def body(flow_start, demand, utility, path_count, cluster_size, incidence, inc_path, inc_edge, capacity, dual_start, partner):
     blocks, paths = flow_start.shape
     incs, _, width = incidence.shape
@@ -290,18 +296,19 @@
     norm_bound = max(2, incs * incs * paths * width // (1024 * edges * blocks))
     unit = float(max(1, incs * paths // (160 * edges)))
     dims = (clusters, shards, blocks, paths, incs, edges, slots, norm_bound, unit)
-    scalars = (path_count, cluster_size, inc_path, inc_edge, partner)
+    scalars = (path_count, inc_path, inc_edge, partner)
     arrays = (flow_start, demand, utility, incidence, capacity, dual_start)
     dma = pltpu.SemaphoreType.DMA
     message = pltpu.VMEM((shards, 8, 128), F32)
     near = pltpu.VMEM((16, 8, 128), F32)
-    return pl.pallas_call(
+    results = pl.pallas_call(
         functools.partial(kernel, dims),
-        out_shape=(jax.ShapeDtypeStruct(flow_start.shape, F32), jax.ShapeDtypeStruct(capacity.shape, F32)),
-        in_specs=[pl.BlockSpec(memory_space=pltpu.HBM)] * (len(scalars) + len(arrays)),
+        out_shape=(pltpu.VMEM(flow_start.shape, F32), pltpu.VMEM(capacity.shape, F32)),
+        in_specs=[pl.BlockSpec(memory_space=pltpu.SMEM)] + [pl.BlockSpec(memory_space=pltpu.HBM)] * (len(scalars) + len(arrays)),
         out_specs=[pl.BlockSpec(memory_space=pltpu.VMEM)] * 2,
         scratch_shapes=[pltpu.SMEM(x.shape, I32) for x in scalars] + [pltpu.VMEM(x.shape, F32) for x in arrays] + [
             pltpu.VMEM((incs * paths, width), BF16),
+            pltpu.VMEM((width, incs * paths), BF16),
             pltpu.VMEM((128, 512), BF16),
             pltpu.VMEM((512, 128), BF16),
             pltpu.VMEM((128, 128), BF16),
@@ -313,11 +320,18 @@
             pltpu.VMEM((ITERS + 1, clusters, 4, 128), F32),
             pltpu.VMEM((32, 128), F32), pltpu.VMEM((32, 128), F32),
             pltpu.VMEM((2, 32, 128), F32), pltpu.VMEM((2, 32, 128), F32),
-            dma((11,)), dma((6,)), dma(()), dma(()), dma((2,)), dma(()), dma((ITERS + 1,)), dma(()), dma(()),
+            dma((10,)), dma((6,)), dma(()), dma(()), dma((2,)), dma(()), dma((ITERS + 1,)), dma(()), dma(()),
         ],
         compiler_params=pltpu.CompilerParams(
-            collective_id=0, has_side_effects=True, vmem_limit_bytes=60 * 1024 * 1024),
-    )(*scalars, *arrays)
+            collective_id=0, has_side_effects=True, vmem_limit_bytes=24 * 1024 * 1024),
+    )(cluster_size, *(pltpu.with_memory_space_constraint(x, pltpu.HBM) for x in scalars + arrays))
+    return pl.pallas_call(
+        write_out,
+        out_shape=(jax.ShapeDtypeStruct(flow_start.shape, F32), jax.ShapeDtypeStruct(capacity.shape, F32)),
+        in_specs=[pl.BlockSpec(memory_space=pltpu.VMEM)] * 2,
+        out_specs=[pl.BlockSpec(memory_space=pltpu.HBM)] * 2,
+        scratch_shapes=[dma((2,))],
+    )(*(pltpu.with_memory_space_constraint(x, pltpu.VMEM) for x in results))
 
 
 def solution(mesh):

time: 79.7 us -> 75.7 us (0.950)
  local copies, waits for them, and re-layouts: 2.59 us -> 0 us
  Pallas kernels: 75.5 us -> 74.3 us
    unnamed x2 -> x0, local copies, waits for them, and re-layouts: 2.59 us -> none
    pallas_call x1 -> x2, Pallas kernels: 75.5 us -> 74.3 us  [the longest x1 73.7 us: body(): pl.pallas_call(functools.partial(kernel, dims), out_shape=(pltpu.VMEM(flo...]
where the time goes in v4:
time: 75.7 us; the launch traced here: 75.6 us
  Pallas kernels  74.3 us (98%)
  between operations  1.29 us (2%)
    pallas_call x1, Pallas kernels, body(): pl.pallas_call(functools.partial(kernel, dims), out_shape=(pltpu.VMEM(flo...  73.7 us

profile of v4, /device:TPU:1, one launch (start us, length us, event | category | flops | bytes accessed | tf_op | source)
XLA Modules:
  0.0 75.6 jit_solution(16441543780094473523)
XLA Ops:
  1.3 73.7 %shard_map.122 = (f32[16,256]{1,0:T(8,128)S(1)}, f32[7,128]{1,0:T(8,128)S(1)}) custom-call(s32[1]{0:T(128)S(6)} %copy.13.cluster_size, s32[16]{0:T(128)} %path_count_hbm.1, s32[32]{0:T(128)} %inc_path_hbm.1, s32[32]{0:T(128)} %inc_edge_hbm.1, s32[1,3]{1,0:T(1,128)} %partner_hbm.1, f32[16,256]{1,0:T(8,128)} %flow_start_hbm.1, f32[16,256]{1,0:T(8,128)} %demand_hbm.1, ...), custom_call_target="tpu_custom_call" | custom-call | tf_op jit(solution)/shard_map/pallas_call | solution.py:304
  75.0 0.6 shard_map.123

commit v5 on v4

--- a/solution.py
+++ b/solution.py
@@ -52,26 +52,47 @@
     flow_start, demand, utility, incidence, capacity, dual_start,
     inc, inc_t, slot_edge, slot_edge_t, choose, choose_t,
     ask_send, ask_recv, flow_send, flow_recv, sum_send, sum_recv,
-    edge_send, edge_recv, border_send, border_recv, start_send, start_recv, rest_send, rest_recv,
-    load_sem, send_sem, ask_sem, flow_sem, sum_sem, edge_sem, border_sem, start_sem, rest_sem,
+    edge_send, edge_recv, border_send, border_recv, own_start, own_bounds, state, bounds, final,
+    load_sem, spread_send, share_send, edge_sent, border_sent, start_sent, bounds_sent, final_sent,
+    ask_sem, flow_sem, sum_sem, edge_sem, border_sem, start_sem, bounds_sem, final_sem,
 ):
     clusters, shards, blocks, paths, incs, edges, slots, norm_bound, unit = dims
     step_size = 1.0 / (2.0 * norm_bound)
     cluster, shard = lax.axis_index("cluster"), lax.axis_index("shard")
     interior = edges - slots
 
+    core = lax.rem(cluster, 2)
+    even = cluster - core
+    host = even + 1
+
     barrier = pltpu.get_barrier_semaphore()
 
-    def greet_shard(k, _):
-        pl.semaphore_signal(barrier, inc=1, device_id=(cluster, lax.rem(shard + k, shards)), device_id_type=MESH)
+    def greet(peer_cluster, peer_shard):
+        pl.semaphore_signal(barrier, inc=1, device_id=(peer_cluster, peer_shard), device_id_type=MESH)
+
+    def greet_hosts(k, _):
+        greet(host, lax.rem(shard + k, shards))
         return 0
 
+    def greet_even(k, _):
+        greet(even, lax.rem(shard + k, shards))
+        return 0
+
     def greet_cluster(k, _):
-        pl.semaphore_signal(barrier, inc=1, device_id=(lax.rem(cluster + k, clusters), shard), device_id_type=MESH)
+        greet(lax.rem(cluster + k + 1 - core, clusters), shard)
         return 0
 
-    lax.fori_loop(1, shards, greet_shard, 0)
-    lax.fori_loop(1, clusters, greet_cluster, 0)
+    lax.fori_loop(1, shards, greet_hosts, 0)
+
+    @pl.when(core == 0)
+    def _():
+        greet(host, shard)
+
+    @pl.when(core == 1)
+    def _():
+        lax.fori_loop(0, shards, greet_even, 0)
+
+    lax.fori_loop(1, clusters - 1, greet_cluster, 0)
 
     loads = [
         pltpu.make_async_copy(src, dst, load_sem.at[n])
@@ -93,33 +114,43 @@
 
     far = [other_end(index) for index in near]
 
-    def send(src, dst, send_to, recv_to, peer):
-        pltpu.make_async_remote_copy(
-            src_ref=src, dst_ref=dst, send_sem=send_to, recv_sem=recv_to,
-            device_id=(cluster, peer), device_id_type=MESH).start()
-
-    def to_all(src, dst, send_to, recv_to):
+    def remote(src, dst, sent, arrived, peer_cluster, peer_shard):
+        return pltpu.make_async_remote_copy(
+            src_ref=src, dst_ref=dst, send_sem=sent, recv_sem=arrived,
+            device_id=(peer_cluster, peer_shard), device_id_type=MESH)
+
+    def to_hosts(src, dst, arrived):
         for u in FAR_FIRST:
             peer, place = (near[u], BACK[u]) if u < 16 else (far[u - 16], 16 + BACK[u - 16])
-            send(src.at[u], dst.at[place], send_to, recv_to, peer)
-
-    def to_near(src, dst, send_to, recv_to):
-        for u in NEAR_FAR_FIRST:
-            send(src.at[u], dst.at[BACK[u]], send_to, recv_to, near[u])
-
-    def to_clusters(src, dst, send_to, recv_to):
+            remote(src.at[u], dst.at[place], spread_send, arrived, host, peer).start()
+
+        @pl.when(core == 0)
+        def _():
+            remote(src.at[0], dst.at[0], spread_send, arrived, host, shard).start()
+
+        @pl.when(core == 1)
+        def _():
+            dst[0] = src[0]
+
+    def to_clusters(src, dst, sent, arrived):
         for k in (4, 3, 5, 2, 6, 1, 7):
-            pltpu.make_async_remote_copy(
-                src_ref=src, dst_ref=dst.at[cluster], send_sem=send_to, recv_sem=recv_to,
-                device_id=(lax.rem(cluster + k, clusters), shard), device_id_type=MESH).start()
+            remote(src, dst.at[cluster], sent, arrived, lax.rem(cluster + k, clusters), shard).start()
         dst[cluster] = src[...]
 
-    def wait(dst, send_to, recv_to):
-        whole = pltpu.make_async_remote_copy(
-            src_ref=dst, dst_ref=dst, send_sem=send_to, recv_sem=recv_to,
-            device_id=(cluster, far[0]), device_id_type=MESH)
-        whole.wait_recv()
-        whole.wait_send()
+    def wait_recv(dst, arrived):
+        remote(dst, dst, spread_send, arrived, cluster, far[0]).wait_recv()
+
+    def wait_send(src, sent):
+        remote(src, src, sent, final_sem, cluster, far[0]).wait_send()
+
+    def hosts_reached(src):
+        @pl.when(core == 0)
+        def _():
+            wait_send(src, spread_send)
+
+        @pl.when(core == 1)
+        def _():
+            wait_send(src.at[pl.ds(0, shards - 1)], spread_send)
 
     tile_role = iota((8, 128), 0) >> 2
     rows, lanes = iota((128, 128), 0), iota((128, 128), 1)
@@ -165,18 +196,26 @@
         count = jnp.where((row32 & 15) == b, path_count[b], count)
     live = (((row32 & 15) < cluster_size[0]) & ((row32 >> 4) * 128 + iota((32, 128), 1) < count)).astype(F32)
     top = halves(demand) * live
-    start = jnp.minimum(jnp.maximum(halves(flow_start), 0.0), top)
-    gain = halves(utility)
-    start_send[...] = start
-    rest_send[0] = top
-    rest_send[1] = gain
-
-    pl.semaphore_wait(barrier, shards + clusters - 2)
-    send(start_send, start_recv, send_sem.at[4], start_sem, far[0])
-    to_all(ask_send, ask_recv, send_sem.at[0], ask_sem)
-    ask_recv[0] = ask_send[0]
-    to_clusters(edge_send, edge_recv, send_sem.at[1], edge_sem)
-    send(rest_send, rest_recv, send_sem.at[5], rest_sem, far[0])
+    own_start[...] = jnp.minimum(jnp.maximum(halves(flow_start), 0.0), top)
+    own_bounds[0] = top
+    own_bounds[1] = halves(utility)
+
+    def to_both(src, dst, sent, arrived):
+        remote(src, dst.at[core, 1], sent.at[1], arrived.at[core, 1], host, far[0]).start()
+
+        @pl.when(core == 0)
+        def _():
+            remote(src, dst.at[core, 0], sent.at[0], arrived.at[core, 0], host, shard).start()
+
+        @pl.when(core == 1)
+        def _():
+            dst[core, 0] = src[...]
+
+    pl.semaphore_wait(barrier, shards + clusters - 2 + (shards - 1) * core)
+    to_both(own_start, state, start_sent, start_sem)
+    to_hosts(ask_send, ask_recv.at[core], ask_sem.at[core])
+    to_clusters(edge_send, edge_recv, edge_sent, edge_sem)
+    to_both(own_bounds, bounds, bounds_sent, bounds_sem)
 
     loads[7].wait()
     lane_q = iota((1, 512), 1)
@@ -205,23 +244,48 @@
         return 0
     lax.fori_loop(0, incs, shrink, 0)
 
-    wait(ask_recv.at[pl.ds(0, shards - 1)], send_sem.at[0], ask_sem)
-    asked = ask_recv[...].reshape(256, 128)
-    rows2, lanes2 = iota((256, 128), 0), iota((256, 128), 1)
-    chosen = ((asked == (lanes2 & 15).astype(F32)) & (((lanes2 >> 4) & 1) == (rows2 & 1))
-              & ((lanes2 >> 5) == ((rows2 >> 2) & 1))).astype(F32)
-    choose[...] = chosen[:128].astype(BF16)
-    choose_t[...] = chosen.T.astype(BF16)
-
-    def share(flows):
-        x = pick(choose[:, :64], flows)
+    def from_holders(src, c, arrived):
+        wait_recv(src if c == 0 else src.at[pl.ds(0, shards - 1)], arrived)
+
+    def share(c, flows):
+        x = pick(choose[c, :, :64], flows)
         for q in range(16):
-            flow_send[q] = x[q * 8:q * 8 + 8]
-        to_near(flow_send, flow_recv, send_sem.at[2], flow_sem)
-        flow_recv[0] = flow_send[0]
+            flow_send[c, q] = x[q * 8:q * 8 + 8]
+        for u in NEAR_FAR_FIRST + ([0] if c == 0 else []):
+            remote(flow_send.at[c, u], flow_recv.at[BACK[u]], share_send.at[c], flow_sem, even + c, near[u]).start()
+        if c == 1:
+            flow_recv[0] = flow_send[c, 0]
+
+    def shared():
+        for c in range(2):
+            wait_send(flow_send.at[c] if c == 0 else flow_send.at[c, pl.ds(0, 15)], share_send.at[c])
+
+    @pl.when(core == 1)
+    def _():
+        rows2, lanes2 = iota((256, 128), 0), iota((256, 128), 1)
+        fit = (((lanes2 >> 4) & 1) == (rows2 & 1)) & ((lanes2 >> 5) == ((rows2 >> 2) & 1))
+        block_of_lane = (lanes2 & 15).astype(F32)
+        for c in range(2):
+            from_holders(ask_recv.at[c], c, ask_sem.at[c])
+            chosen = ((ask_recv[c].reshape(256, 128) == block_of_lane) & fit).astype(F32)
+            choose[c] = chosen[:128].astype(BF16)
+            choose_t[c] = chosen.T.astype(BF16)
+            for role in range(c, 2):
+                wait_recv(state.at[c, role], start_sem.at[c, role])
+            share(c, state[c].reshape(64, 128))
+        for c in range(2):
+            for role in range(c, 2):
+                wait_recv(bounds.at[c, role], bounds_sem.at[c, role])
 
     def total_load(t):
-        wait(flow_recv.at[pl.ds(0, 15)], send_sem.at[2], flow_sem)
+        @pl.when(core == 0)
+        def _():
+            wait_recv(flow_recv, flow_sem)
+
+        @pl.when(core == 1)
+        def _():
+            wait_recv(flow_recv.at[pl.ds(0, 15)], flow_sem)
+
         got = flow_recv[...].reshape(128, 128)
         parts = dot(slot_edge_t[...], jnp.concatenate(thirds(got), axis=1))
         columns = []
@@ -231,8 +295,8 @@
         sums = dot(jnp.concatenate(columns, axis=1), inc[...])
         own = (sums[16:] + sums[8:16]) + sums[:8]
         border_send[...] = own[:4]
-        to_clusters(border_send, border_recv.at[t], send_sem.at[3], border_sem.at[t])
-        wait(border_recv.at[t, pl.ds(0, clusters - 1)], send_sem.at[3], border_sem.at[t])
+        to_clusters(border_send, border_recv.at[t], border_sent, border_sem.at[t])
+        wait_recv(border_recv.at[t, pl.ds(0, clusters - 1)], border_sem.at[t])
         twin = jnp.zeros((4, 128), F32)
         for c in range(clusters):
             twin = twin + jnp.where(partner_row == c, border_recv[t, c], 0.0)
@@ -243,14 +307,7 @@
         duals = (duals + load) - split
         return (load - split) + duals, duals
 
-    wait(start_recv, send_sem.at[4], start_sem)
-    flows = jnp.concatenate([start, start_recv[...]], axis=0)
-    share(flows)
-
-    wait(rest_recv, send_sem.at[5], rest_sem)
-    top = jnp.concatenate([top, rest_recv[0]], axis=0)
-    gain = jnp.concatenate([gain, rest_recv[1]], axis=0)
-    wait(edge_recv.at[pl.ds(0, clusters - 1)], send_sem.at[1], edge_sem)
+    wait_recv(edge_recv.at[pl.ds(0, clusters - 1)], edge_sem)
     twin = jnp.zeros((8, 128), F32)
     for c in range(clusters):
         twin = twin + jnp.where(partner8 == c, edge_recv[c], 0.0)
@@ -259,24 +316,60 @@
 
     residual, duals = settle(total_load(0), duals)
 
+    hosts_reached(ask_send)
+    wait_send(edge_recv.at[pl.ds(0, clusters - 1)], edge_sent)
+    for src, sem in ((own_start, start_sent), (own_bounds, bounds_sent)):
+        wait_send(src, sem.at[1])
+
+        @pl.when(core == 0)
+        def _():
+            wait_send(src, sem.at[0])
+
     def iterate(t, carry):
-        flows, residual, duals = carry
+        residual, duals = carry
         turn = lax.rem(t, 2)
         parts = dot(jnp.concatenate(thirds(residual), axis=0), inc_t[...])
         back = (parts[16:] + parts[8:16]) + parts[:8]
         back = jnp.concatenate([back[:, q * 128:q * 128 + 128] for q in range(2 * incs)], axis=0)
         fill(sum_send, pick(slot_edge[...], back))
-        to_all(sum_send, sum_recv.at[turn], send_sem.at[0], sum_sem.at[turn])
-        sum_recv[turn, 0] = sum_send[0]
-        wait(sum_recv.at[turn, pl.ds(0, shards - 1)], send_sem.at[0], sum_sem.at[turn])
-        grad = pick(choose_t[:64, :], sum_recv[turn].reshape(256, 128))
-        flows = jnp.minimum(jnp.maximum(flows - step_size * (grad - gain), 0.0), top)
-        share(flows)
-        residual, duals = settle(total_load(t), duals)
-        return flows, residual, duals
-
-    flows, residual, duals = lax.fori_loop(1, ITERS + 1, iterate, (flows, residual, duals))
-    flows_out[...] = jnp.concatenate([flows[:16], flows[16:32]], axis=1)
+        to_hosts(sum_send, sum_recv.at[turn, core], sum_sem.at[turn, core])
+        wait_send(border_recv.at[t, pl.ds(0, clusters - 1)], border_sent)
+
+        @pl.when(core == 1)
+        def _():
+            shared()
+            for c in range(2):
+                from_holders(sum_recv.at[turn, c], c, sum_sem.at[turn, c])
+                grad = pick(choose_t[c, :64, :], sum_recv[turn, c].reshape(256, 128))
+                top = bounds[c, :, 0].reshape(64, 128)
+                gain = bounds[c, :, 1].reshape(64, 128)
+                flows = state[c].reshape(64, 128)
+                flows = jnp.minimum(jnp.maximum(flows - step_size * (grad - gain), 0.0), top)
+                state[c] = flows.reshape(2, 32, 128)
+                share(c, flows)
+
+            @pl.when(t == ITERS)
+            def _():
+                remote(state.at[0, 0], final, final_sent, final_sem, even, shard).start()
+
+        hosts_reached(sum_send)
+        return settle(total_load(t), duals)
+
+    residual, duals = lax.fori_loop(1, ITERS + 1, iterate, (residual, duals))
+    wait_send(border_recv.at[0, pl.ds(0, clusters - 1)], border_sent)
+
+    @pl.when(core == 0)
+    def _():
+        wait_recv(final, final_sem)
+
+    @pl.when(core == 1)
+    def _():
+        shared()
+        wait_send(state.at[0, 0], final_sent)
+        final[...] = state[1, 0]
+
+    flows = final[...]
+    flows_out[...] = jnp.concatenate([flows[:16], flows[16:]], axis=1)
     duals_out[...] = jnp.concatenate([duals[4:], duals[:slots]], axis=0)
 
 
@@ -299,8 +392,6 @@
     scalars = (path_count, inc_path, inc_edge, partner)
     arrays = (flow_start, demand, utility, incidence, capacity, dual_start)
     dma = pltpu.SemaphoreType.DMA
-    message = pltpu.VMEM((shards, 8, 128), F32)
-    near = pltpu.VMEM((16, 8, 128), F32)
     results = pl.pallas_call(
         functools.partial(kernel, dims),
         out_shape=(pltpu.VMEM(flow_start.shape, F32), pltpu.VMEM(capacity.shape, F32)),
@@ -311,16 +402,25 @@
             pltpu.VMEM((width, incs * paths), BF16),
             pltpu.VMEM((128, 512), BF16),
             pltpu.VMEM((512, 128), BF16),
-            pltpu.VMEM((128, 128), BF16),
-            pltpu.VMEM((128, 256), BF16),
-            message, message, near, near, message, pltpu.VMEM((2, shards, 8, 128), F32),
+            pltpu.VMEM((2, 128, 128), BF16),
+            pltpu.VMEM((2, 128, 256), BF16),
+            pltpu.VMEM((shards, 8, 128), F32),
+            pltpu.VMEM((2, shards, 8, 128), F32),
+            pltpu.VMEM((2, 16, 8, 128), F32),
+            pltpu.VMEM((16, 8, 128), F32),
+            pltpu.VMEM((shards, 8, 128), F32),
+            pltpu.VMEM((2, 2, shards, 8, 128), F32),
             pltpu.VMEM((8, 128), F32),
             pltpu.VMEM((clusters, 8, 128), F32),
             pltpu.VMEM((4, 128), F32),
             pltpu.VMEM((ITERS + 1, clusters, 4, 128), F32),
-            pltpu.VMEM((32, 128), F32), pltpu.VMEM((32, 128), F32),
-            pltpu.VMEM((2, 32, 128), F32), pltpu.VMEM((2, 32, 128), F32),
-            dma((10,)), dma((6,)), dma(()), dma(()), dma((2,)), dma(()), dma((ITERS + 1,)), dma(()), dma(()),
+            pltpu.VMEM((32, 128), F32),
+            pltpu.VMEM((2, 32, 128), F32),
+            pltpu.VMEM((2, 2, 32, 128), F32),
+            pltpu.VMEM((2, 2, 2, 32, 128), F32),
+            pltpu.VMEM((32, 128), F32),
+            dma((10,)), dma(()), dma((2,)), dma(()), dma(()), dma((2,)), dma((2,)), dma(()),
+            dma((2,)), dma(()), dma((2, 2)), dma(()), dma((ITERS + 1,)), dma((2, 2)), dma((2, 2)), dma(()),
         ],
         compiler_params=pltpu.CompilerParams(
             collective_id=0, has_side_effects=True, vmem_limit_bytes=24 * 1024 * 1024),

time: 75.7 us -> 72.6 us (0.959)
  Pallas kernels: 74.3 us -> 71.2 us
    pallas_call x1, Pallas kernels: 73.7 us -> 70.6 us  [body(): pl.pallas_call(functools.partial(kernel, dims), out_shape=(pltpu.VMEM(flo...]
where the time goes in v5:
time: 72.6 us; the launch traced here: 72.5 us
  Pallas kernels  71.2 us (98%)
  between operations  1.29 us (2%)
    pallas_call x1, Pallas kernels, body(): pl.pallas_call(functools.partial(kernel, dims), out_shape=(pltpu.VMEM(flo...  70.6 us

profile of v5, /device:TPU:1, one launch (start us, length us, event | category | flops | bytes accessed | tf_op | source)
XLA Modules:
  0.0 72.5 jit_solution(13771969740658828701)
XLA Ops:
  1.3 70.6 %shard_map.122 = (f32[16,256]{1,0:T(8,128)S(1)}, f32[7,128]{1,0:T(8,128)S(1)}) custom-call(s32[1]{0:T(128)S(6)} %copy.13.cluster_size, s32[16]{0:T(128)} %path_count_hbm.1, s32[32]{0:T(128)} %inc_path_hbm.1, s32[32]{0:T(128)} %inc_edge_hbm.1, s32[1,3]{1,0:T(1,128)} %partner_hbm.1, f32[16,256]{1,0:T(8,128)} %flow_start_hbm.1, f32[16,256]{1,0:T(8,128)} %demand_hbm.1, ...), custom_call_target="tpu_custom_call" | custom-call | tf_op jit(solution)/shard_map/pallas_call | solution.py:395
  71.9 0.6 shard_map.123

commit v6 on v5

--- a/solution.py
+++ b/solution.py
@@ -39,8 +39,19 @@
 
 NEAR = sorted(((x, z, y) for x in range(4) for z in range(2) for y in range(4) if hops((x, z, y)) <= 2), key=hops)
 BACK = [NEAR.index(tuple(-d % n for d, n in zip(offset, GRID))) for offset in NEAR]
-FAR_FIRST = sorted(range(1, 32), key=lambda u: -(hops(NEAR[u]) if u < 16 else 5 - hops(NEAR[u - 16])))
+
+
+def distance(u):
+    return hops(NEAR[u]) if u < 16 else 5 - hops(NEAR[u - 16])
+
+
+def place_x(u):
+    return NEAR[u][0] if u < 16 else (NEAR[u - 16][0] + 2) % 4
+
+
+FAR_FIRST = sorted(range(1, 32), key=lambda u: (-distance(u), -min(place_x(u), 4 - place_x(u))))
 NEAR_FAR_FIRST = [u for u in FAR_FIRST if u < 16]
+DISTANT = [u for u in FAR_FIRST if u >= 16]
 
 
 def kernel(
@@ -54,7 +65,7 @@
     ask_send, ask_recv, flow_send, flow_recv, sum_send, sum_recv,
     edge_send, edge_recv, border_send, border_recv, own_start, own_bounds, state, bounds, final,
     load_sem, spread_send, share_send, edge_sent, border_sent, start_sent, bounds_sent, final_sent,
-    ask_sem, flow_sem, sum_sem, edge_sem, border_sem, start_sem, bounds_sem, final_sem,
+    ask_sem, distant_sem, flow_sem, sum_sem, edge_sem, border_sem, start_sem, bounds_sem, final_sem,
 ):
     clusters, shards, blocks, paths, incs, edges, slots, norm_bound, unit = dims
     step_size = 1.0 / (2.0 * norm_bound)
@@ -119,11 +130,12 @@
             src_ref=src, dst_ref=dst, send_sem=sent, recv_sem=arrived,
             device_id=(peer_cluster, peer_shard), device_id_type=MESH)
 
-    def to_hosts(src, dst, arrived):
-        for u in FAR_FIRST:
+    def to_hosts(places, src, dst, arrived):
+        for u in places:
             peer, place = (near[u], BACK[u]) if u < 16 else (far[u - 16], 16 + BACK[u - 16])
             remote(src.at[u], dst.at[place], spread_send, arrived, host, peer).start()
 
+    def to_own_host(src, dst, arrived):
         @pl.when(core == 0)
         def _():
             remote(src.at[0], dst.at[0], spread_send, arrived, host, shard).start()
@@ -213,8 +225,10 @@
 
     pl.semaphore_wait(barrier, shards + clusters - 2 + (shards - 1) * core)
     to_both(own_start, state, start_sent, start_sem)
-    to_hosts(ask_send, ask_recv.at[core], ask_sem.at[core])
+    to_hosts(NEAR_FAR_FIRST, ask_send, ask_recv.at[core], ask_sem.at[core])
+    to_own_host(ask_send, ask_recv.at[core], ask_sem.at[core])
     to_clusters(edge_send, edge_recv, edge_sent, edge_sem)
+    to_hosts(DISTANT, ask_send, ask_recv.at[core], distant_sem.at[core])
     to_both(own_bounds, bounds, bounds_sent, bounds_sem)
 
     loads[7].wait()
@@ -266,14 +280,17 @@
         fit = (((lanes2 >> 4) & 1) == (rows2 & 1)) & ((lanes2 >> 5) == ((rows2 >> 2) & 1))
         block_of_lane = (lanes2 & 15).astype(F32)
         for c in range(2):
-            from_holders(ask_recv.at[c], c, ask_sem.at[c])
-            chosen = ((ask_recv[c].reshape(256, 128) == block_of_lane) & fit).astype(F32)
-            choose[c] = chosen[:128].astype(BF16)
-            choose_t[c] = chosen.T.astype(BF16)
+            wait_recv(ask_recv.at[c, pl.ds(0, 16 - c)], ask_sem.at[c])
+            chosen = (ask_recv[c, :16].reshape(128, 128) == block_of_lane[:128]) & fit[:128]
+            choose[c] = chosen.astype(F32).astype(BF16)
+        for c in range(2):
             for role in range(c, 2):
                 wait_recv(state.at[c, role], start_sem.at[c, role])
             share(c, state[c].reshape(64, 128))
         for c in range(2):
+            wait_recv(ask_recv.at[c, pl.ds(16, 16)], distant_sem.at[c])
+            chosen = (ask_recv[c].reshape(256, 128) == block_of_lane) & fit
+            choose_t[c] = chosen.astype(F32).T.astype(BF16)
             for role in range(c, 2):
                 wait_recv(bounds.at[c, role], bounds_sem.at[c, role])
 
@@ -332,7 +349,8 @@
         back = (parts[16:] + parts[8:16]) + parts[:8]
         back = jnp.concatenate([back[:, q * 128:q * 128 + 128] for q in range(2 * incs)], axis=0)
         fill(sum_send, pick(slot_edge[...], back))
-        to_hosts(sum_send, sum_recv.at[turn, core], sum_sem.at[turn, core])
+        to_hosts(FAR_FIRST, sum_send, sum_recv.at[turn, core], sum_sem.at[turn, core])
+        to_own_host(sum_send, sum_recv.at[turn, core], sum_sem.at[turn, core])
         wait_send(border_recv.at[t, pl.ds(0, clusters - 1)], border_sent)
 
         @pl.when(core == 1)
@@ -420,7 +438,7 @@
             pltpu.VMEM((2, 2, 2, 32, 128), F32),
             pltpu.VMEM((32, 128), F32),
             dma((10,)), dma(()), dma((2,)), dma(()), dma(()), dma((2,)), dma((2,)), dma(()),
-            dma((2,)), dma(()), dma((2, 2)), dma(()), dma((ITERS + 1,)), dma((2, 2)), dma((2, 2)), dma(()),
+            dma((2,)), dma((2,)), dma(()), dma((2, 2)), dma(()), dma((ITERS + 1,)), dma((2, 2)), dma((2, 2)), dma(()),
         ],
         compiler_params=pltpu.CompilerParams(
             collective_id=0, has_side_effects=True, vmem_limit_bytes=24 * 1024 * 1024),

time: 72.6 us -> 71.7 us (0.988)
  Pallas kernels: 71.2 us -> 70.3 us
    pallas_call x1, Pallas kernels: 70.6 us -> 69.7 us  [body(): pl.pallas_call(functools.partial(kernel, dims), out_shape=(pltpu.VMEM(flo...]
where the time goes in v6:
time: 71.7 us; the launch traced here: 71.6 us
  Pallas kernels  70.3 us (98%)
  between operations  1.29 us (2%)
    pallas_call x1, Pallas kernels, body(): pl.pallas_call(functools.partial(kernel, dims), out_shape=(pltpu.VMEM(flo...  69.7 us

profile of v6, /device:TPU:1, one launch (start us, length us, event | category | flops | bytes accessed | tf_op | source)
XLA Modules:
  0.0 71.6 jit_solution(2572456701511111913)
XLA Ops:
  1.3 69.7 %shard_map.122 = (f32[16,256]{1,0:T(8,128)S(1)}, f32[7,128]{1,0:T(8,128)S(1)}) custom-call(s32[1]{0:T(128)S(6)} %copy.13.cluster_size, s32[16]{0:T(128)} %path_count_hbm.1, s32[32]{0:T(128)} %inc_path_hbm.1, s32[32]{0:T(128)} %inc_edge_hbm.1, s32[1,3]{1,0:T(1,128)} %partner_hbm.1, f32[16,256]{1,0:T(8,128)} %flow_start_hbm.1, f32[16,256]{1,0:T(8,128)} %demand_hbm.1, ...), custom_call_target="tpu_custom_call" | custom-call | tf_op jit(solution)/shard_map/pallas_call | solution.py:413
  71.0 0.6 shard_map.123

commit v7 on v6

--- a/solution.py
+++ b/solution.py
@@ -30,7 +30,8 @@
 
 def pick(selector, x):
     high, mid, low = thirds(x)
-    return (dot(selector, low) + dot(selector, mid)) + dot(selector, high)
+    x = dot(selector, jnp.concatenate([low, mid, high], axis=1))
+    return (x[:, :128] + x[:, 128:256]) + x[:, 256:]
 
 
 def hops(offset):
@@ -228,8 +229,6 @@
     to_hosts(NEAR_FAR_FIRST, ask_send, ask_recv.at[core], ask_sem.at[core])
     to_own_host(ask_send, ask_recv.at[core], ask_sem.at[core])
     to_clusters(edge_send, edge_recv, edge_sent, edge_sem)
-    to_hosts(DISTANT, ask_send, ask_recv.at[core], distant_sem.at[core])
-    to_both(own_bounds, bounds, bounds_sent, bounds_sem)
 
     loads[7].wait()
     lane_q = iota((1, 512), 1)
@@ -247,6 +246,9 @@
     for k in range(slots):
         partner_row = jnp.where(iota((4, 128), 0) == k, partner[0, k], partner_row)
     partner8 = jnp.concatenate([partner_row, partner_row], axis=0)
+
+    to_hosts(DISTANT, ask_send, ask_recv.at[core], distant_sem.at[core])
+    to_both(own_bounds, bounds, bounds_sent, bounds_sem)
 
     loads[9].wait()
 
@@ -363,8 +365,8 @@
                 gain = bounds[c, :, 1].reshape(64, 128)
                 flows = state[c].reshape(64, 128)
                 flows = jnp.minimum(jnp.maximum(flows - step_size * (grad - gain), 0.0), top)
+                share(c, flows)
                 state[c] = flows.reshape(2, 32, 128)
-                share(c, flows)
 
             @pl.when(t == ITERS)
             def _():

time: 71.7 us -> 71.4 us (level)
  no operation moved by 1% of the time
where the time goes in v7:
time: 71.4 us; the launch traced here: 71.3 us
  Pallas kernels  70 us (98%)
  between operations  1.29 us (2%)
    pallas_call x1, Pallas kernels, body(): pl.pallas_call(functools.partial(kernel, dims), out_shape=(pltpu.VMEM(flo...  69.4 us

profile of v7, /device:TPU:1, one launch (start us, length us, event | category | flops | bytes accessed | tf_op | source)
XLA Modules:
  0.0 71.3 jit_solution(14501567536552854750)
XLA Ops:
  1.3 69.4 %shard_map.122 = (f32[16,256]{1,0:T(8,128)S(1)}, f32[7,128]{1,0:T(8,128)S(1)}) custom-call(s32[1]{0:T(128)S(6)} %copy.13.cluster_size, s32[16]{0:T(128)} %path_count_hbm.1, s32[32]{0:T(128)} %inc_path_hbm.1, s32[32]{0:T(128)} %inc_edge_hbm.1, s32[1,3]{1,0:T(1,128)} %partner_hbm.1, f32[16,256]{1,0:T(8,128)} %flow_start_hbm.1, f32[16,256]{1,0:T(8,128)} %demand_hbm.1, ...), custom_call_target="tpu_custom_call" | custom-call | tf_op jit(solution)/shard_map/pallas_call | solution.py:415
  70.7 0.6 shard_map.123

commit v8 on v7

--- a/solution.py
+++ b/solution.py
@@ -350,8 +350,13 @@
         parts = dot(jnp.concatenate(thirds(residual), axis=0), inc_t[...])
         back = (parts[16:] + parts[8:16]) + parts[:8]
         back = jnp.concatenate([back[:, q * 128:q * 128 + 128] for q in range(2 * incs)], axis=0)
-        fill(sum_send, pick(slot_edge[...], back))
-        to_hosts(FAR_FIRST, sum_send, sum_recv.at[turn, core], sum_sem.at[turn, core])
+        sums = pick(slot_edge[...], back)
+        for q in range(16):
+            sum_send[16 + q] = pltpu.roll(sums[q * 8:q * 8 + 8], 4, 0)
+        to_hosts(DISTANT, sum_send, sum_recv.at[turn, core], sum_sem.at[turn, core])
+        for q in range(16):
+            sum_send[q] = sums[q * 8:q * 8 + 8]
+        to_hosts(NEAR_FAR_FIRST, sum_send, sum_recv.at[turn, core], sum_sem.at[turn, core])
         to_own_host(sum_send, sum_recv.at[turn, core], sum_sem.at[turn, core])
         wait_send(border_recv.at[t, pl.ds(0, clusters - 1)], border_sent)
 

time: 71.4 us -> 71.4 us (level)
  no operation moved by 1% of the time
where the time goes in v8:
time: 71.4 us; the launch traced here: 71.3 us
  Pallas kernels  70 us (98%)
  between operations  1.29 us (2%)
    pallas_call x1, Pallas kernels, body(): pl.pallas_call(functools.partial(kernel, dims), out_shape=(pltpu.VMEM(flo...  69.4 us

profile of v8, /device:TPU:1, one launch (start us, length us, event | category | flops | bytes accessed | tf_op | source)
XLA Modules:
  0.0 71.3 jit_solution(1902202242167842653)
XLA Ops:
  1.3 69.4 %shard_map.122 = (f32[16,256]{1,0:T(8,128)S(1)}, f32[7,128]{1,0:T(8,128)S(1)}) custom-call(s32[1]{0:T(128)S(6)} %copy.13.cluster_size, s32[16]{0:T(128)} %path_count_hbm.1, s32[32]{0:T(128)} %inc_path_hbm.1, s32[32]{0:T(128)} %inc_edge_hbm.1, s32[1,3]{1,0:T(1,128)} %partner_hbm.1, f32[16,256]{1,0:T(8,128)} %flow_start_hbm.1, f32[16,256]{1,0:T(8,128)} %demand_hbm.1, ...), custom_call_target="tpu_custom_call" | custom-call | tf_op jit(solution)/shard_map/pallas_call | solution.py:420
  70.7 0.6 shard_map.123

commit v9 on v8

--- a/solution.py
+++ b/solution.py
@@ -265,12 +265,14 @@
 
     def share(c, flows):
         x = pick(choose[c, :, :64], flows)
-        for q in range(16):
-            flow_send[c, q] = x[q * 8:q * 8 + 8]
-        for u in NEAR_FAR_FIRST + ([0] if c == 0 else []):
-            remote(flow_send.at[c, u], flow_recv.at[BACK[u]], share_send.at[c], flow_sem, even + c, near[u]).start()
-        if c == 1:
-            flow_recv[0] = flow_send[c, 0]
+        for places in ([u for u in NEAR_FAR_FIRST if distance(u) == 2], [u for u in NEAR_FAR_FIRST if distance(u) == 1] + [0]):
+            for u in places:
+                flow_send[c, u] = x[u * 8:u * 8 + 8]
+            for u in places:
+                if u == 0 and c == 1:
+                    flow_recv[0] = x[:8]
+                else:
+                    remote(flow_send.at[c, u], flow_recv.at[BACK[u]], share_send.at[c], flow_sem, even + c, near[u]).start()
 
     def shared():
         for c in range(2):

time: 71.4 us -> 71.4 us (level)
  no operation moved by 1% of the time
where the time goes in v9:
time: 71.4 us; the launch traced here: 71.3 us
  Pallas kernels  70 us (98%)
  between operations  1.29 us (2%)
    pallas_call x1, Pallas kernels, body(): pl.pallas_call(functools.partial(kernel, dims), out_shape=(pltpu.VMEM(flo...  69.4 us

profile of v9, /device:TPU:1, one launch (start us, length us, event | category | flops | bytes accessed | tf_op | source)
XLA Modules:
  0.0 71.3 jit_solution(1613796240838752281)
XLA Ops:
  1.3 69.4 %shard_map.122 = (f32[16,256]{1,0:T(8,128)S(1)}, f32[7,128]{1,0:T(8,128)S(1)}) custom-call(s32[1]{0:T(128)S(6)} %copy.13.cluster_size, s32[16]{0:T(128)} %path_count_hbm.1, s32[32]{0:T(128)} %inc_path_hbm.1, s32[32]{0:T(128)} %inc_edge_hbm.1, s32[1,3]{1,0:T(1,128)} %partner_hbm.1, f32[16,256]{1,0:T(8,128)} %flow_start_hbm.1, f32[16,256]{1,0:T(8,128)} %demand_hbm.1, ...), custom_call_target="tpu_custom_call" | custom-call | tf_op jit(solution)/shard_map/pallas_call | solution.py:422
  70.7 0.6 shard_map.123

commit v10 on v8

--- a/solution.py
+++ b/solution.py
@@ -363,7 +363,7 @@
         @pl.when(core == 1)
         def _():
             shared()
-            for c in range(2):
+            for c in (1, 0):
                 from_holders(sum_recv.at[turn, c], c, sum_sem.at[turn, c])
                 grad = pick(choose_t[c, :64, :], sum_recv[turn, c].reshape(256, 128))
                 top = bounds[c, :, 0].reshape(64, 128)

time: 71.4 us -> 71.4 us (level)
  no operation moved by 1% of the time
where the time goes in v10:
time: 71.4 us; the launch traced here: 71.3 us
  Pallas kernels  70 us (98%)
  between operations  1.29 us (2%)
    pallas_call x1, Pallas kernels, body(): pl.pallas_call(functools.partial(kernel, dims), out_shape=(pltpu.VMEM(flo...  69.4 us

profile of v10, /device:TPU:1, one launch (start us, length us, event | category | flops | bytes accessed | tf_op | source)
XLA Modules:
  0.0 71.3 jit_solution(7995220123847435248)
XLA Ops:
  1.3 69.4 %shard_map.122 = (f32[16,256]{1,0:T(8,128)S(1)}, f32[7,128]{1,0:T(8,128)S(1)}) custom-call(s32[1]{0:T(128)S(6)} %copy.13.cluster_size, s32[16]{0:T(128)} %path_count_hbm.1, s32[32]{0:T(128)} %inc_path_hbm.1, s32[32]{0:T(128)} %inc_edge_hbm.1, s32[1,3]{1,0:T(1,128)} %partner_hbm.1, f32[16,256]{1,0:T(8,128)} %flow_start_hbm.1, f32[16,256]{1,0:T(8,128)} %demand_hbm.1, ...), custom_call_target="tpu_custom_call" | custom-call | tf_op jit(solution)/shard_map/pallas_call | solution.py:420
  70.7 0.6 shard_map.123
